TPU v7x, 256 devices: a whole 4x4x8 slice. The times are simulated.
256 devices in a mesh: segment: 4 (over y), dom: 64 (over z, x, core).
Axes of the slice: x: 4, y: 4, z: 8, core: 2. Of those that a mesh axis runs over, the one named last changes fastest.
Arguments:
- features: bfloat16 [4, 32768, 512], P(None, 'dom'), may hold values from -6 to 6
- layer_weights: bfloat16 [8, 1024, 512], P('segment'), may hold values from -0.1875 to 0.1875
- layer_bias: float32 [8, 512], P('segment'), may hold values from -3 to 3
- layer_gain: float32 [8, 512], P('segment'), may hold values from 0.1 to 1.9
- tile_val: bfloat16 [256, 4, 128, 128], P('dom'), may hold values from -0.25 to 0.25
- tile_col: int32 [256, 4], P('dom'), may hold values from 0 to 3
- tile_count: int32 [256], P('dom'), may hold values from 1 to 4, as said below
- cross_val: bfloat16 [8, 256, 128, 128], P('segment', 'dom'), may hold values from -0.5 to 0.5
- send_rows: int32 [8, 8192], P('segment', 'dom'), may hold values from 0 to 511, as said below
Outputs:
- segment_out: bfloat16 [4, 4, 32768, 512], P('segment', None, 'dom')
Inputs may be any that keep to these rules, and one draw needn't show every extreme that they name: `tile_count`: in some row block of the graph all 4 slots are live. `send_rows`: each partition's list at a layer holds 128 distinct local node indices and contains 512 - 1.
All inputs are finite; a program needn't handle non-finite values.
Results may differ from a plain program's by a relative error of at most 0.012.
Values may be sent and summed in bfloat16 or wider, within the bound.
A program may use at most 64 MiB of HBM per device.

v0:
```python
import jax
import jax.numpy as jnp
from jax import lax
from jax.sharding import PartitionSpec as P

LS = 2


def from_partner(x, axis, apart):
    return lax.ppermute(x, axis, [(i, i ^ 1 << apart) for i in range(lax.axis_size(axis))])


def shifted(value, axis, steps):
    count = lax.axis_size(axis)
    leading, last = (max(0, -steps), min(count, count - steps))
    return lax.ppermute(value, axis, [(source, source + steps) for source in range(leading, last)])


def layer_step(h, weights, bias, gain, cross, rows, position, tile_val, tile_col, tile_count):
    hf = h.astype(jnp.float32)
    meansq = jnp.mean(hf * hf, axis=-1, keepdims=True)
    x = (hf * lax.rsqrt(meansq + 1e-05) * gain).astype(jnp.bfloat16)
    sent = jnp.take(x, rows, axis=0)
    nbits = lax.axis_size("dom").bit_length() - 1
    bit = position * (nbits - 1) // max(LS - 1, 1)
    recv = from_partner(sent, "dom", bit)
    nblocks = tile_col.shape[0]
    width = x.shape[1]
    blocks = x.reshape(nblocks, tile_val.shape[2], width)
    most = jnp.max(tile_count)

    def slot_step(slot, acc):
        cols = lax.dynamic_index_in_dim(tile_col, slot, 1, keepdims=False)
        source = jnp.take(blocks, cols, axis=0)
        tiles = lax.dynamic_index_in_dim(tile_val, slot, 1, keepdims=False)
        live = (slot < tile_count)[:, None, None]
        prod = jnp.einsum("bij,bjd->bid", tiles, source, preferred_element_type=jnp.float32)
        return acc + jnp.where(live, prod, jnp.float32(0.0))

    acc = lax.fori_loop(0, most, slot_step, jnp.zeros(blocks.shape, jnp.float32))
    acc = acc + jnp.einsum("bir,rd->bid", cross, recv, preferred_element_type=jnp.float32)
    agg = acc.reshape(x.shape).astype(jnp.bfloat16)
    z = jnp.dot(x, weights[:width], preferred_element_type=jnp.float32)
    z = z + jnp.dot(agg, weights[width:], preferred_element_type=jnp.float32)
    z = z + bias
    return (hf + jax.nn.silu(z)).astype(jnp.bfloat16)


def run_section(h, weights, bias, gain, cross, rows, first, tile_val, tile_col, tile_count):
    for position in range(LS):
        layer = first + position
        h = layer_step(
            h,
            weights[layer],
            bias[layer],
            gain[layer],
            cross[layer],
            rows[layer],
            position,
            tile_val,
            tile_col,
            tile_count,
        )
    return h


def shards(
    features,
    layer_weights,
    layer_bias,
    layer_gain,
    tile_val,
    tile_col,
    tile_count,
    cross_val,
    send_rows,
):
    sections = lax.axis_size("segment")
    segment_id = lax.axis_index("segment")
    micro = features.shape[0]

    def tick(step, carry):
        incoming, stored = carry
        feed = lax.dynamic_index_in_dim(features, jnp.clip(step, 0, micro - 1), 0, keepdims=False)
        h = jnp.where(segment_id == 0, feed, incoming)
        h = run_section(
            h,
            layer_weights,
            layer_bias,
            layer_gain,
            cross_val,
            send_rows,
            0,
            tile_val,
            tile_col,
            tile_count,
        )
        which = step - segment_id
        valid = (which >= 0) & (which < micro)
        place = jnp.clip(which, 0, micro - 1)
        before = lax.dynamic_index_in_dim(stored, place, 0, keepdims=False)
        stored = lax.dynamic_update_index_in_dim(stored, jnp.where(valid, h, before), place, 0)
        passed = shifted(h, "segment", 1)
        return (passed, stored)

    start = (jnp.zeros(features.shape[1:], jnp.bfloat16), jnp.zeros(features.shape, jnp.bfloat16))
    finals = lax.fori_loop(0, micro + sections - 1, tick, start)
    return finals[1][None]


def solution(mesh):
    in_specs = (
        P(None, "dom", None),
        P("segment", None, None),
        P("segment", None),
        P("segment", None),
        P("dom", None, None, None),
        P("dom", None),
        P("dom"),
        P("segment", "dom", None, None),
        P("segment", "dom"),
    )
    out_specs = P("segment", None, "dom", None)
    return jax.shard_map(shards, mesh=mesh, in_specs=in_specs, out_specs=out_specs, check_vma=False)
```

profile of v0, /device:TPU:86, one launch (start us, length us, event | category | flops | bytes accessed | tf_op | source)
XLA Modules:
  0.0 420.9 jit_solution(5062968498473962611)
XLA Ops:
  4.8 416.0 %while.68 = (s32[]{:T(128)}, bf16[512,512]{1,0:T(8,128)(2,1)S(1)}, bf16[4,512,512]{2,1,0:T(8,128)(2,1)}, pred[]{:T(512)}, bf16[4,512,512]{2,1,0:T(8,128)(2,1)}, ...) while((s32[]{:T(128)}, bf16[512,512]{1,0:T(8,128)(2,1)S(1)}, ...), condition=%wide.region_8.11_spmd, body=%wide.region_1.10_spmd.sunk | while | flops 1353849344 | bytes 44432368 | solution.py:107
  9.2 8.1 %while.69 = (s32[]{:T(128)}, f32[4,128,512]{2,1,0:T(8,128)S(1)}, s32[]{:T(128)}, s32[4]{0:T(128)S(1)}, bf16[4,4,128,128]{3,2,0,1:T(8,128)(2,1)S(1)}, /*index=5*/...) while((s32[]{:T(128)}, f32[4,128,512]{2,1,0:T(8,128)S(1)}, ...), condition=%wide.region_4.5_spmd, body=%wide.region_3.4_spmd.sunk | while | flops 67896352 | bytes 3807011 | solution.py:40
  24.9 5.7 %while.70 = (s32[]{:T(128)}, f32[4,128,512]{2,1,0:T(8,128)S(1)}, s32[]{:T(128)}, s32[4]{0:T(128)S(1)}, bf16[4,4,128,128]{3,2,0,1:T(8,128)(2,1)S(1)}, /*index=5*/...) while((s32[]{:T(128)}, f32[4,128,512]{2,1,0:T(8,128)S(1)}, ...), condition=%wide.region_7.9_spmd, body=%wide.region_6.8_spmd.sunk | while | flops 67896352 | bytes 3806443 | solution.py:40
  31.6 9.6 %collective-permute-start.1 = (bf16[128,512]{1,0:T(8,128)(2,1)S(1)}, bf16[128,512]{1,0:T(8,128)(2,1)S(1)}, u32[]{:S(2)}, u32[]{:S(2)}) collective-permute-start(bf16[128,512]{1,0:T(8,128)(2,1)S(1)} %broadcast_select_fusion.5), channel_id=1, source_target_pairs={{0,32},{1,33},{2,34},{3,35},{4,36},{5,37},{6,38},{7,39},{8,40},{9,... | collective-permute-start | bytes 393224 | tf_op jit(solution)/shard_map/while/body/eval_jaxpr/ppermute | solution.py:10
  42.7 4.8 %collective-permute-done.1 = bf16[128,512]{1,0:T(8,128)(2,1)S(1)} collective-permute-done((bf16[128,512]{1,0:T(8,128)(2,1)S(1)}, bf16[128,512]{1,0:T(8,128)(2,1)S(1)}, u32[]{:S(2)}, u32[]{:S(2)}) %collective-permute-start.1) | collective-permute-done | bytes 131104 | tf_op jit(solution)/shard_map/while/body/eval_jaxpr/ppermute | solution.py:10
  50.5 3.2 collective-permute-start.2
  53.6 12.6 %collective-permute-done.2 = bf16[512,512]{1,0:T(8,128)(2,1)S(1)} collective-permute-done((bf16[512,512]{1,0:T(8,128)(2,1)S(1)}, bf16[512,512]{1,0:T(8,128)(2,1)S(1)}, u32[]{:S(2)}, u32[]{:S(2)}) %collective-permute-start.2) | collective-permute-done | bytes 524320 | tf_op jit(solution)/shard_map/while/body/eval_jaxpr/ppermute | solution.py:16
  70.7 8.1 %while.69 = (s32[]{:T(128)}, f32[4,128,512]{2,1,0:T(8,128)S(1)}, s32[]{:T(128)}, s32[4]{0:T(128)S(1)}, bf16[4,4,128,128]{3,2,0,1:T(8,128)(2,1)S(1)}, /*index=5*/...) while((s32[]{:T(128)}, f32[4,128,512]{2,1,0:T(8,128)S(1)}, ...), condition=%wide.region_4.5_spmd, body=%wide.region_3.4_spmd.sunk | while | flops 67896352 | bytes 3807011 | solution.py:40
  86.3 5.7 %while.70 = (s32[]{:T(128)}, f32[4,128,512]{2,1,0:T(8,128)S(1)}, s32[]{:T(128)}, s32[4]{0:T(128)S(1)}, bf16[4,4,128,128]{3,2,0,1:T(8,128)(2,1)S(1)}, /*index=5*/...) while((s32[]{:T(128)}, f32[4,128,512]{2,1,0:T(8,128)S(1)}, ...), condition=%wide.region_7.9_spmd, body=%wide.region_6.8_spmd.sunk | while | flops 67896352 | bytes 3806443 | solution.py:40
  93.0 7.3 %collective-permute-start.1 = (bf16[128,512]{1,0:T(8,128)(2,1)S(1)}, bf16[128,512]{1,0:T(8,128)(2,1)S(1)}, u32[]{:S(2)}, u32[]{:S(2)}) collective-permute-start(bf16[128,512]{1,0:T(8,128)(2,1)S(1)} %broadcast_select_fusion.5), channel_id=1, source_target_pairs={{0,32},{1,33},{2,34},{3,35},{4,36},{5,37},{6,38},{7,39},{8,40},{9,... | collective-permute-start | bytes 393224 | tf_op jit(solution)/shard_map/while/body/eval_jaxpr/ppermute | solution.py:10
  101.8 4.8 %collective-permute-done.1 = bf16[128,512]{1,0:T(8,128)(2,1)S(1)} collective-permute-done((bf16[128,512]{1,0:T(8,128)(2,1)S(1)}, bf16[128,512]{1,0:T(8,128)(2,1)S(1)}, u32[]{:S(2)}, u32[]{:S(2)}) %collective-permute-start.1) | collective-permute-done | bytes 131104 | tf_op jit(solution)/shard_map/while/body/eval_jaxpr/ppermute | solution.py:10
  107.0 2.6 bitcast_dynamic-update-slice_fusion.2
  109.5 3.2 collective-permute-start.2
  112.7 12.6 %collective-permute-done.2 = bf16[512,512]{1,0:T(8,128)(2,1)S(1)} collective-permute-done((bf16[512,512]{1,0:T(8,128)(2,1)S(1)}, bf16[512,512]{1,0:T(8,128)(2,1)S(1)}, u32[]{:S(2)}, u32[]{:S(2)}) %collective-permute-start.2) | collective-permute-done | bytes 524320 | tf_op jit(solution)/shard_map/while/body/eval_jaxpr/ppermute | solution.py:16
  129.8 8.1 %while.69 = (s32[]{:T(128)}, f32[4,128,512]{2,1,0:T(8,128)S(1)}, s32[]{:T(128)}, s32[4]{0:T(128)S(1)}, bf16[4,4,128,128]{3,2,0,1:T(8,128)(2,1)S(1)}, /*index=5*/...) while((s32[]{:T(128)}, f32[4,128,512]{2,1,0:T(8,128)S(1)}, ...), condition=%wide.region_4.5_spmd, body=%wide.region_3.4_spmd.sunk | while | flops 67896352 | bytes 3807011 | solution.py:40
  145.4 5.7 %while.70 = (s32[]{:T(128)}, f32[4,128,512]{2,1,0:T(8,128)S(1)}, s32[]{:T(128)}, s32[4]{0:T(128)S(1)}, bf16[4,4,128,128]{3,2,0,1:T(8,128)(2,1)S(1)}, /*index=5*/...) while((s32[]{:T(128)}, f32[4,128,512]{2,1,0:T(8,128)S(1)}, ...), condition=%wide.region_7.9_spmd, body=%wide.region_6.8_spmd.sunk | while | flops 67896352 | bytes 3806443 | solution.py:40
  152.1 7.3 %collective-permute-start.1 = (bf16[128,512]{1,0:T(8,128)(2,1)S(1)}, bf16[128,512]{1,0:T(8,128)(2,1)S(1)}, u32[]{:S(2)}, u32[]{:S(2)}) collective-permute-start(bf16[128,512]{1,0:T(8,128)(2,1)S(1)} %broadcast_select_fusion.5), channel_id=1, source_target_pairs={{0,32},{1,33},{2,34},{3,35},{4,36},{5,37},{6,38},{7,39},{8,40},{9,... | collective-permute-start | bytes 393224 | tf_op jit(solution)/shard_map/while/body/eval_jaxpr/ppermute | solution.py:10
  160.9 4.9 %collective-permute-done.1 = bf16[128,512]{1,0:T(8,128)(2,1)S(1)} collective-permute-done((bf16[128,512]{1,0:T(8,128)(2,1)S(1)}, bf16[128,512]{1,0:T(8,128)(2,1)S(1)}, u32[]{:S(2)}, u32[]{:S(2)}) %collective-permute-start.1) | collective-permute-done | bytes 131104 | tf_op jit(solution)/shard_map/while/body/eval_jaxpr/ppermute | solution.py:10
  166.1 2.6 bitcast_dynamic-update-slice_fusion.2
  168.6 3.2 collective-permute-start.2
  171.8 12.6 %collective-permute-done.2 = bf16[512,512]{1,0:T(8,128)(2,1)S(1)} collective-permute-done((bf16[512,512]{1,0:T(8,128)(2,1)S(1)}, bf16[512,512]{1,0:T(8,128)(2,1)S(1)}, u32[]{:S(2)}, u32[]{:S(2)}) %collective-permute-start.2) | collective-permute-done | bytes 524320 | tf_op jit(solution)/shard_map/while/body/eval_jaxpr/ppermute | solution.py:16
  188.9 8.1 %while.69 = (s32[]{:T(128)}, f32[4,128,512]{2,1,0:T(8,128)S(1)}, s32[]{:T(128)}, s32[4]{0:T(128)S(1)}, bf16[4,4,128,128]{3,2,0,1:T(8,128)(2,1)S(1)}, /*index=5*/...) while((s32[]{:T(128)}, f32[4,128,512]{2,1,0:T(8,128)S(1)}, ...), condition=%wide.region_4.5_spmd, body=%wide.region_3.4_spmd.sunk | while | flops 67896352 | bytes 3807011 | solution.py:40
  204.5 5.7 %while.70 = (s32[]{:T(128)}, f32[4,128,512]{2,1,0:T(8,128)S(1)}, s32[]{:T(128)}, s32[4]{0:T(128)S(1)}, bf16[4,4,128,128]{3,2,0,1:T(8,128)(2,1)S(1)}, /*index=5*/...) while((s32[]{:T(128)}, f32[4,128,512]{2,1,0:T(8,128)S(1)}, ...), condition=%wide.region_7.9_spmd, body=%wide.region_6.8_spmd.sunk | while | flops 67896352 | bytes 3806443 | solution.py:40
  211.2 7.3 %collective-permute-start.1 = (bf16[128,512]{1,0:T(8,128)(2,1)S(1)}, bf16[128,512]{1,0:T(8,128)(2,1)S(1)}, u32[]{:S(2)}, u32[]{:S(2)}) collective-permute-start(bf16[128,512]{1,0:T(8,128)(2,1)S(1)} %broadcast_select_fusion.5), channel_id=1, source_target_pairs={{0,32},{1,33},{2,34},{3,35},{4,36},{5,37},{6,38},{7,39},{8,40},{9,... | collective-permute-start | bytes 393224 | tf_op jit(solution)/shard_map/while/body/eval_jaxpr/ppermute | solution.py:10
  220.0 4.9 %collective-permute-done.1 = bf16[128,512]{1,0:T(8,128)(2,1)S(1)} collective-permute-done((bf16[128,512]{1,0:T(8,128)(2,1)S(1)}, bf16[128,512]{1,0:T(8,128)(2,1)S(1)}, u32[]{:S(2)}, u32[]{:S(2)}) %collective-permute-start.1) | collective-permute-done | bytes 131104 | tf_op jit(solution)/shard_map/while/body/eval_jaxpr/ppermute | solution.py:10
  225.2 2.6 bitcast_dynamic-update-slice_fusion.2
  227.7 3.2 collective-permute-start.2
  230.9 12.6 %collective-permute-done.2 = bf16[512,512]{1,0:T(8,128)(2,1)S(1)} collective-permute-done((bf16[512,512]{1,0:T(8,128)(2,1)S(1)}, bf16[512,512]{1,0:T(8,128)(2,1)S(1)}, u32[]{:S(2)}, u32[]{:S(2)}) %collective-permute-start.2) | collective-permute-done | bytes 524320 | tf_op jit(solution)/shard_map/while/body/eval_jaxpr/ppermute | solution.py:16
  248.0 8.1 %while.69 = (s32[]{:T(128)}, f32[4,128,512]{2,1,0:T(8,128)S(1)}, s32[]{:T(128)}, s32[4]{0:T(128)S(1)}, bf16[4,4,128,128]{3,2,0,1:T(8,128)(2,1)S(1)}, /*index=5*/...) while((s32[]{:T(128)}, f32[4,128,512]{2,1,0:T(8,128)S(1)}, ...), condition=%wide.region_4.5_spmd, body=%wide.region_3.4_spmd.sunk | while | flops 67896352 | bytes 3807011 | solution.py:40
  263.6 5.7 %while.70 = (s32[]{:T(128)}, f32[4,128,512]{2,1,0:T(8,128)S(1)}, s32[]{:T(128)}, s32[4]{0:T(128)S(1)}, bf16[4,4,128,128]{3,2,0,1:T(8,128)(2,1)S(1)}, /*index=5*/...) while((s32[]{:T(128)}, f32[4,128,512]{2,1,0:T(8,128)S(1)}, ...), condition=%wide.region_7.9_spmd, body=%wide.region_6.8_spmd.sunk | while | flops 67896352 | bytes 3806443 | solution.py:40
  270.3 7.3 %collective-permute-start.1 = (bf16[128,512]{1,0:T(8,128)(2,1)S(1)}, bf16[128,512]{1,0:T(8,128)(2,1)S(1)}, u32[]{:S(2)}, u32[]{:S(2)}) collective-permute-start(bf16[128,512]{1,0:T(8,128)(2,1)S(1)} %broadcast_select_fusion.5), channel_id=1, source_target_pairs={{0,32},{1,33},{2,34},{3,35},{4,36},{5,37},{6,38},{7,39},{8,40},{9,... | collective-permute-start | bytes 393224 | tf_op jit(solution)/shard_map/while/body/eval_jaxpr/ppermute | solution.py:10
  279.1 4.9 %collective-permute-done.1 = bf16[128,512]{1,0:T(8,128)(2,1)S(1)} collective-permute-done((bf16[128,512]{1,0:T(8,128)(2,1)S(1)}, bf16[128,512]{1,0:T(8,128)(2,1)S(1)}, u32[]{:S(2)}, u32[]{:S(2)}) %collective-permute-start.1) | collective-permute-done | bytes 131104 | tf_op jit(solution)/shard_map/while/body/eval_jaxpr/ppermute | solution.py:10
  284.3 2.6 bitcast_dynamic-update-slice_fusion.2
  286.8 3.2 collective-permute-start.2
  290.0 12.6 %collective-permute-done.2 = bf16[512,512]{1,0:T(8,128)(2,1)S(1)} collective-permute-done((bf16[512,512]{1,0:T(8,128)(2,1)S(1)}, bf16[512,512]{1,0:T(8,128)(2,1)S(1)}, u32[]{:S(2)}, u32[]{:S(2)}) %collective-permute-start.2) | collective-permute-done | bytes 524320 | tf_op jit(solution)/shard_map/while/body/eval_jaxpr/ppermute | solution.py:16
  307.1 8.1 %while.69 = (s32[]{:T(128)}, f32[4,128,512]{2,1,0:T(8,128)S(1)}, s32[]{:T(128)}, s32[4]{0:T(128)S(1)}, bf16[4,4,128,128]{3,2,0,1:T(8,128)(2,1)S(1)}, /*index=5*/...) while((s32[]{:T(128)}, f32[4,128,512]{2,1,0:T(8,128)S(1)}, ...), condition=%wide.region_4.5_spmd, body=%wide.region_3.4_spmd.sunk | while | flops 67896352 | bytes 3807011 | solution.py:40
  322.7 5.7 %while.70 = (s32[]{:T(128)}, f32[4,128,512]{2,1,0:T(8,128)S(1)}, s32[]{:T(128)}, s32[4]{0:T(128)S(1)}, bf16[4,4,128,128]{3,2,0,1:T(8,128)(2,1)S(1)}, /*index=5*/...) while((s32[]{:T(128)}, f32[4,128,512]{2,1,0:T(8,128)S(1)}, ...), condition=%wide.region_7.9_spmd, body=%wide.region_6.8_spmd.sunk | while | flops 67896352 | bytes 3806443 | solution.py:40
  329.4 7.3 %collective-permute-start.1 = (bf16[128,512]{1,0:T(8,128)(2,1)S(1)}, bf16[128,512]{1,0:T(8,128)(2,1)S(1)}, u32[]{:S(2)}, u32[]{:S(2)}) collective-permute-start(bf16[128,512]{1,0:T(8,128)(2,1)S(1)} %broadcast_select_fusion.5), channel_id=1, source_target_pairs={{0,32},{1,33},{2,34},{3,35},{4,36},{5,37},{6,38},{7,39},{8,40},{9,... | collective-permute-start | bytes 393224 | tf_op jit(solution)/shard_map/while/body/eval_jaxpr/ppermute | solution.py:10
  338.1 4.9 %collective-permute-done.1 = bf16[128,512]{1,0:T(8,128)(2,1)S(1)} collective-permute-done((bf16[128,512]{1,0:T(8,128)(2,1)S(1)}, bf16[128,512]{1,0:T(8,128)(2,1)S(1)}, u32[]{:S(2)}, u32[]{:S(2)}) %collective-permute-start.1) | collective-permute-done | bytes 131104 | tf_op jit(solution)/shard_map/while/body/eval_jaxpr/ppermute | solution.py:10
  343.4 2.6 bitcast_dynamic-update-slice_fusion.2
  345.9 3.2 collective-permute-start.2
  349.1 12.6 %collective-permute-done.2 = bf16[512,512]{1,0:T(8,128)(2,1)S(1)} collective-permute-done((bf16[512,512]{1,0:T(8,128)(2,1)S(1)}, bf16[512,512]{1,0:T(8,128)(2,1)S(1)}, u32[]{:S(2)}, u32[]{:S(2)}) %collective-permute-start.2) | collective-permute-done | bytes 524320 | tf_op jit(solution)/shard_map/while/body/eval_jaxpr/ppermute | solution.py:16
  366.2 8.1 %while.69 = (s32[]{:T(128)}, f32[4,128,512]{2,1,0:T(8,128)S(1)}, s32[]{:T(128)}, s32[4]{0:T(128)S(1)}, bf16[4,4,128,128]{3,2,0,1:T(8,128)(2,1)S(1)}, /*index=5*/...) while((s32[]{:T(128)}, f32[4,128,512]{2,1,0:T(8,128)S(1)}, ...), condition=%wide.region_4.5_spmd, body=%wide.region_3.4_spmd.sunk | while | flops 67896352 | bytes 3807011 | solution.py:40
  381.8 5.7 %while.70 = (s32[]{:T(128)}, f32[4,128,512]{2,1,0:T(8,128)S(1)}, s32[]{:T(128)}, s32[4]{0:T(128)S(1)}, bf16[4,4,128,128]{3,2,0,1:T(8,128)(2,1)S(1)}, /*index=5*/...) while((s32[]{:T(128)}, f32[4,128,512]{2,1,0:T(8,128)S(1)}, ...), condition=%wide.region_7.9_spmd, body=%wide.region_6.8_spmd.sunk | while | flops 67896352 | bytes 3806443 | solution.py:40
  388.5 7.3 %collective-permute-start.1 = (bf16[128,512]{1,0:T(8,128)(2,1)S(1)}, bf16[128,512]{1,0:T(8,128)(2,1)S(1)}, u32[]{:S(2)}, u32[]{:S(2)}) collective-permute-start(bf16[128,512]{1,0:T(8,128)(2,1)S(1)} %broadcast_select_fusion.5), channel_id=1, source_target_pairs={{0,32},{1,33},{2,34},{3,35},{4,36},{5,37},{6,38},{7,39},{8,40},{9,... | collective-permute-start | bytes 393224 | tf_op jit(solution)/shard_map/while/body/eval_jaxpr/ppermute | solution.py:10
  397.2 4.9 %collective-permute-done.1 = bf16[128,512]{1,0:T(8,128)(2,1)S(1)} collective-permute-done((bf16[128,512]{1,0:T(8,128)(2,1)S(1)}, bf16[128,512]{1,0:T(8,128)(2,1)S(1)}, u32[]{:S(2)}, u32[]{:S(2)}) %collective-permute-start.1) | collective-permute-done | bytes 131104 | tf_op jit(solution)/shard_map/while/body/eval_jaxpr/ppermute | solution.py:10
  405.0 3.2 collective-permute-start.2
  408.2 12.6 %collective-permute-done.2 = bf16[512,512]{1,0:T(8,128)(2,1)S(1)} collective-permute-done((bf16[512,512]{1,0:T(8,128)(2,1)S(1)}, bf16[512,512]{1,0:T(8,128)(2,1)S(1)}, u32[]{:S(2)}, u32[]{:S(2)}) %collective-permute-start.2) | collective-permute-done | bytes 524320 | tf_op jit(solution)/shard_map/while/body/eval_jaxpr/ppermute | solution.py:16
  (598 shorter events, 170.6 us)
Async XLA Ops:
  9.1 12.7 %collective-permute-start = (bf16[128,512]{1,0:T(8,128)(2,1)}, bf16[128,512]{1,0:T(8,128)(2,1)S(1)}, u32[]{:S(2)}, u32[]{:S(2)}) collective-permute-start(bf16[128,512]{1,0:T(8,128)(2,1)} %broadcast_select_fusion.4), channel_id=1, source_target_pairs={{0,1},{1,0},{2,3},{3,2},{4,5},{5,4},{6,7},{7,6},{8,9},{9,8},{10,11... | collective-permute-start | bytes 393224 | tf_op jit(solution)/shard_map/while/body/eval_jaxpr/ppermute | solution.py:10
  31.4 16.4 %copy-start.2 = (bf16[512,512]{1,0:T(8,128)(2,1)S(1)}, bf16[512,512]{1,0:T(8,128)(2,1)}, u32[]{:S(2)}) copy-start(bf16[512,512]{1,0:T(8,128)(2,1)} %copy-done.1) | copy-start | bytes 1572868 | tf_op jit(solution)/shard_map/while
  31.4 16.4 %copy-start.3 = (bf16[1,512,512]{2,1,0:T(8,128)(2,1)S(1)}, bf16[1,512,512]{2,1,0:T(8,128)(2,1)}, u32[]{:S(2)}) copy-start(bf16[1,512,512]{2,1,0:T(8,128)(2,1)} %constant_dynamic-slice_fusion.2) | copy-start | bytes 1572868 | tf_op jit(solution)/shard_map/while
  31.5 16.4 %copy-start.15 = (f32[1,512]{1,0:T(1,128)S(1)}, f32[1,512]{1,0:T(1,128)}, u32[]{:S(2)}) copy-start(f32[1,512]{1,0:T(1,128)} %get-tuple-element.671) | copy-start | bytes 6148 | tf_op jit(solution)/shard_map/while
  31.6 16.0 %collective-permute-start.1 = (bf16[128,512]{1,0:T(8,128)(2,1)S(1)}, bf16[128,512]{1,0:T(8,128)(2,1)S(1)}, u32[]{:S(2)}, u32[]{:S(2)}) collective-permute-start(bf16[128,512]{1,0:T(8,128)(2,1)S(1)} %broadcast_select_fusion.5), channel_id=1, source_target_pairs={{0,32},{1,33},{2,34},{3,35},{4,36},{5,37},{6,38},{7,39},{8,40},{9,... | collective-permute-start | bytes 393224 | tf_op jit(solution)/shard_map/while/body/eval_jaxpr/ppermute | solution.py:10
  47.8 18.4 %copy-start.10 = (f32[2,512]{1,0:T(2,128)S(1)}, f32[2,512]{1,0:T(2,128)}, u32[]{:S(2)}) copy-start(f32[2,512]{1,0:T(2,128)} %get-tuple-element.912) | copy-start | bytes 12292 | tf_op jit(solution)/shard_map/while
  47.9 18.4 %copy-start.12 = (f32[2,512]{1,0:T(2,128)S(1)}, f32[2,512]{1,0:T(2,128)}, u32[]{:S(2)}) copy-start(f32[2,512]{1,0:T(2,128)} %get-tuple-element.941) | copy-start | bytes 12292 | tf_op jit(solution)/shard_map/while
  47.9 18.4 %copy-start.18 = (s32[2,128]{1,0:T(2,128)S(1)}, s32[2,128]{1,0:T(2,128)}, u32[]{:S(2)}) copy-start(s32[2,128]{1,0:T(2,128)} %get-tuple-element.971) | copy-start | bytes 3076 | tf_op jit(solution)/shard_map/while
  50.5 15.8 %collective-permute-start.2 = (bf16[512,512]{1,0:T(8,128)(2,1)S(1)}, bf16[512,512]{1,0:T(8,128)(2,1)S(1)}, u32[]{:S(2)}, u32[]{:S(2)}) collective-permute-start(bf16[512,512]{1,0:T(8,128)(2,1)S(1)} %get-tuple-element.685), channel_id=1, source_target_pairs={{0,64},{64,128},{128,192},{1,65},{65,129},{129,193},{2,66},{66,130... | collective-permute-start | bytes 1572872 | tf_op jit(solution)/shard_map/while/body/eval_jaxpr/ppermute | solution.py:16
  70.5 12.7 %collective-permute-start = (bf16[128,512]{1,0:T(8,128)(2,1)}, bf16[128,512]{1,0:T(8,128)(2,1)S(1)}, u32[]{:S(2)}, u32[]{:S(2)}) collective-permute-start(bf16[128,512]{1,0:T(8,128)(2,1)} %broadcast_select_fusion.4), channel_id=1, source_target_pairs={{0,1},{1,0},{2,3},{3,2},{4,5},{5,4},{6,7},{7,6},{8,9},{9,8},{10,11... | collective-permute-start | bytes 393224 | tf_op jit(solution)/shard_map/while/body/eval_jaxpr/ppermute | solution.py:10
  93.0 13.6 %collective-permute-start.1 = (bf16[128,512]{1,0:T(8,128)(2,1)S(1)}, bf16[128,512]{1,0:T(8,128)(2,1)S(1)}, u32[]{:S(2)}, u32[]{:S(2)}) collective-permute-start(bf16[128,512]{1,0:T(8,128)(2,1)S(1)} %broadcast_select_fusion.5), channel_id=1, source_target_pairs={{0,32},{1,33},{2,34},{3,35},{4,36},{5,37},{6,38},{7,39},{8,40},{9,... | collective-permute-start | bytes 393224 | tf_op jit(solution)/shard_map/while/body/eval_jaxpr/ppermute | solution.py:10
  106.9 18.4 %copy-start.10 = (f32[2,512]{1,0:T(2,128)S(1)}, f32[2,512]{1,0:T(2,128)}, u32[]{:S(2)}) copy-start(f32[2,512]{1,0:T(2,128)} %get-tuple-element.912) | copy-start | bytes 12292 | tf_op jit(solution)/shard_map/while
  106.9 18.4 %copy-start.12 = (f32[2,512]{1,0:T(2,128)S(1)}, f32[2,512]{1,0:T(2,128)}, u32[]{:S(2)}) copy-start(f32[2,512]{1,0:T(2,128)} %get-tuple-element.941) | copy-start | bytes 12292 | tf_op jit(solution)/shard_map/while
  107.0 18.4 %copy-start.18 = (s32[2,128]{1,0:T(2,128)S(1)}, s32[2,128]{1,0:T(2,128)}, u32[]{:S(2)}) copy-start(s32[2,128]{1,0:T(2,128)} %get-tuple-element.971) | copy-start | bytes 3076 | tf_op jit(solution)/shard_map/while
  109.5 15.8 %collective-permute-start.2 = (bf16[512,512]{1,0:T(8,128)(2,1)S(1)}, bf16[512,512]{1,0:T(8,128)(2,1)S(1)}, u32[]{:S(2)}, u32[]{:S(2)}) collective-permute-start(bf16[512,512]{1,0:T(8,128)(2,1)S(1)} %get-tuple-element.685), channel_id=1, source_target_pairs={{0,64},{64,128},{128,192},{1,65},{65,129},{129,193},{2,66},{66,130... | collective-permute-start | bytes 1572872 | tf_op jit(solution)/shard_map/while/body/eval_jaxpr/ppermute | solution.py:16
  129.6 12.7 %collective-permute-start = (bf16[128,512]{1,0:T(8,128)(2,1)}, bf16[128,512]{1,0:T(8,128)(2,1)S(1)}, u32[]{:S(2)}, u32[]{:S(2)}) collective-permute-start(bf16[128,512]{1,0:T(8,128)(2,1)} %broadcast_select_fusion.4), channel_id=1, source_target_pairs={{0,1},{1,0},{2,3},{3,2},{4,5},{5,4},{6,7},{7,6},{8,9},{9,8},{10,11... | collective-permute-start | bytes 393224 | tf_op jit(solution)/shard_map/while/body/eval_jaxpr/ppermute | solution.py:10
  152.0 14.0 %copy-start.2 = (bf16[512,512]{1,0:T(8,128)(2,1)S(1)}, bf16[512,512]{1,0:T(8,128)(2,1)}, u32[]{:S(2)}) copy-start(bf16[512,512]{1,0:T(8,128)(2,1)} %copy-done.1) | copy-start | bytes 1572868 | tf_op jit(solution)/shard_map/while
  152.0 14.0 %copy-start.3 = (bf16[1,512,512]{2,1,0:T(8,128)(2,1)S(1)}, bf16[1,512,512]{2,1,0:T(8,128)(2,1)}, u32[]{:S(2)}) copy-start(bf16[1,512,512]{2,1,0:T(8,128)(2,1)} %constant_dynamic-slice_fusion.2) | copy-start | bytes 1572868 | tf_op jit(solution)/shard_map/while
  152.0 14.0 %copy-start.15 = (f32[1,512]{1,0:T(1,128)S(1)}, f32[1,512]{1,0:T(1,128)}, u32[]{:S(2)}) copy-start(f32[1,512]{1,0:T(1,128)} %get-tuple-element.671) | copy-start | bytes 6148 | tf_op jit(solution)/shard_map/while
  152.1 13.6 %collective-permute-start.1 = (bf16[128,512]{1,0:T(8,128)(2,1)S(1)}, bf16[128,512]{1,0:T(8,128)(2,1)S(1)}, u32[]{:S(2)}, u32[]{:S(2)}) collective-permute-start(bf16[128,512]{1,0:T(8,128)(2,1)S(1)} %broadcast_select_fusion.5), channel_id=1, source_target_pairs={{0,32},{1,33},{2,34},{3,35},{4,36},{5,37},{6,38},{7,39},{8,40},{9,... | collective-permute-start | bytes 393224 | tf_op jit(solution)/shard_map/while/body/eval_jaxpr/ppermute | solution.py:10
  166.0 18.4 %copy-start.10 = (f32[2,512]{1,0:T(2,128)S(1)}, f32[2,512]{1,0:T(2,128)}, u32[]{:S(2)}) copy-start(f32[2,512]{1,0:T(2,128)} %get-tuple-element.912) | copy-start | bytes 12292 | tf_op jit(solution)/shard_map/while
  166.0 18.4 %copy-start.12 = (f32[2,512]{1,0:T(2,128)S(1)}, f32[2,512]{1,0:T(2,128)}, u32[]{:S(2)}) copy-start(f32[2,512]{1,0:T(2,128)} %get-tuple-element.941) | copy-start | bytes 12292 | tf_op jit(solution)/shard_map/while
  166.1 18.4 %copy-start.18 = (s32[2,128]{1,0:T(2,128)S(1)}, s32[2,128]{1,0:T(2,128)}, u32[]{:S(2)}) copy-start(s32[2,128]{1,0:T(2,128)} %get-tuple-element.971) | copy-start | bytes 3076 | tf_op jit(solution)/shard_map/while
  168.6 15.8 %collective-permute-start.2 = (bf16[512,512]{1,0:T(8,128)(2,1)S(1)}, bf16[512,512]{1,0:T(8,128)(2,1)S(1)}, u32[]{:S(2)}, u32[]{:S(2)}) collective-permute-start(bf16[512,512]{1,0:T(8,128)(2,1)S(1)} %get-tuple-element.685), channel_id=1, source_target_pairs={{0,64},{64,128},{128,192},{1,65},{65,129},{129,193},{2,66},{66,130... | collective-permute-start | bytes 1572872 | tf_op jit(solution)/shard_map/while/body/eval_jaxpr/ppermute | solution.py:16
  188.7 12.7 %collective-permute-start = (bf16[128,512]{1,0:T(8,128)(2,1)}, bf16[128,512]{1,0:T(8,128)(2,1)S(1)}, u32[]{:S(2)}, u32[]{:S(2)}) collective-permute-start(bf16[128,512]{1,0:T(8,128)(2,1)} %broadcast_select_fusion.4), channel_id=1, source_target_pairs={{0,1},{1,0},{2,3},{3,2},{4,5},{5,4},{6,7},{7,6},{8,9},{9,8},{10,11... | collective-permute-start | bytes 393224 | tf_op jit(solution)/shard_map/while/body/eval_jaxpr/ppermute | solution.py:10
  211.2 13.6 %collective-permute-start.1 = (bf16[128,512]{1,0:T(8,128)(2,1)S(1)}, bf16[128,512]{1,0:T(8,128)(2,1)S(1)}, u32[]{:S(2)}, u32[]{:S(2)}) collective-permute-start(bf16[128,512]{1,0:T(8,128)(2,1)S(1)} %broadcast_select_fusion.5), channel_id=1, source_target_pairs={{0,32},{1,33},{2,34},{3,35},{4,36},{5,37},{6,38},{7,39},{8,40},{9,... | collective-permute-start | bytes 393224 | tf_op jit(solution)/shard_map/while/body/eval_jaxpr/ppermute | solution.py:10
  225.1 18.4 %copy-start.10 = (f32[2,512]{1,0:T(2,128)S(1)}, f32[2,512]{1,0:T(2,128)}, u32[]{:S(2)}) copy-start(f32[2,512]{1,0:T(2,128)} %get-tuple-element.912) | copy-start | bytes 12292 | tf_op jit(solution)/shard_map/while
  225.1 18.4 %copy-start.12 = (f32[2,512]{1,0:T(2,128)S(1)}, f32[2,512]{1,0:T(2,128)}, u32[]{:S(2)}) copy-start(f32[2,512]{1,0:T(2,128)} %get-tuple-element.941) | copy-start | bytes 12292 | tf_op jit(solution)/shard_map/while
  225.2 18.4 %copy-start.18 = (s32[2,128]{1,0:T(2,128)S(1)}, s32[2,128]{1,0:T(2,128)}, u32[]{:S(2)}) copy-start(s32[2,128]{1,0:T(2,128)} %get-tuple-element.971) | copy-start | bytes 3076 | tf_op jit(solution)/shard_map/while
  227.7 15.8 %collective-permute-start.2 = (bf16[512,512]{1,0:T(8,128)(2,1)S(1)}, bf16[512,512]{1,0:T(8,128)(2,1)S(1)}, u32[]{:S(2)}, u32[]{:S(2)}) collective-permute-start(bf16[512,512]{1,0:T(8,128)(2,1)S(1)} %get-tuple-element.685), channel_id=1, source_target_pairs={{0,64},{64,128},{128,192},{1,65},{65,129},{129,193},{2,66},{66,130... | collective-permute-start | bytes 1572872 | tf_op jit(solution)/shard_map/while/body/eval_jaxpr/ppermute | solution.py:16
  247.8 12.7 %collective-permute-start = (bf16[128,512]{1,0:T(8,128)(2,1)}, bf16[128,512]{1,0:T(8,128)(2,1)S(1)}, u32[]{:S(2)}, u32[]{:S(2)}) collective-permute-start(bf16[128,512]{1,0:T(8,128)(2,1)} %broadcast_select_fusion.4), channel_id=1, source_target_pairs={{0,1},{1,0},{2,3},{3,2},{4,5},{5,4},{6,7},{7,6},{8,9},{9,8},{10,11... | collective-permute-start | bytes 393224 | tf_op jit(solution)/shard_map/while/body/eval_jaxpr/ppermute | solution.py:10
  270.3 13.6 %collective-permute-start.1 = (bf16[128,512]{1,0:T(8,128)(2,1)S(1)}, bf16[128,512]{1,0:T(8,128)(2,1)S(1)}, u32[]{:S(2)}, u32[]{:S(2)}) collective-permute-start(bf16[128,512]{1,0:T(8,128)(2,1)S(1)} %broadcast_select_fusion.5), channel_id=1, source_target_pairs={{0,32},{1,33},{2,34},{3,35},{4,36},{5,37},{6,38},{7,39},{8,40},{9,... | collective-permute-start | bytes 393224 | tf_op jit(solution)/shard_map/while/body/eval_jaxpr/ppermute | solution.py:10
  284.2 18.4 %copy-start.10 = (f32[2,512]{1,0:T(2,128)S(1)}, f32[2,512]{1,0:T(2,128)}, u32[]{:S(2)}) copy-start(f32[2,512]{1,0:T(2,128)} %get-tuple-element.912) | copy-start | bytes 12292 | tf_op jit(solution)/shard_map/while
  284.2 18.4 %copy-start.12 = (f32[2,512]{1,0:T(2,128)S(1)}, f32[2,512]{1,0:T(2,128)}, u32[]{:S(2)}) copy-start(f32[2,512]{1,0:T(2,128)} %get-tuple-element.941) | copy-start | bytes 12292 | tf_op jit(solution)/shard_map/while
  284.3 18.4 %copy-start.18 = (s32[2,128]{1,0:T(2,128)S(1)}, s32[2,128]{1,0:T(2,128)}, u32[]{:S(2)}) copy-start(s32[2,128]{1,0:T(2,128)} %get-tuple-element.971) | copy-start | bytes 3076 | tf_op jit(solution)/shard_map/while
  286.8 15.8 %collective-permute-start.2 = (bf16[512,512]{1,0:T(8,128)(2,1)S(1)}, bf16[512,512]{1,0:T(8,128)(2,1)S(1)}, u32[]{:S(2)}, u32[]{:S(2)}) collective-permute-start(bf16[512,512]{1,0:T(8,128)(2,1)S(1)} %get-tuple-element.685), channel_id=1, source_target_pairs={{0,64},{64,128},{128,192},{1,65},{65,129},{129,193},{2,66},{66,130... | collective-permute-start | bytes 1572872 | tf_op jit(solution)/shard_map/while/body/eval_jaxpr/ppermute | solution.py:16
  306.9 12.7 %collective-permute-start = (bf16[128,512]{1,0:T(8,128)(2,1)}, bf16[128,512]{1,0:T(8,128)(2,1)S(1)}, u32[]{:S(2)}, u32[]{:S(2)}) collective-permute-start(bf16[128,512]{1,0:T(8,128)(2,1)} %broadcast_select_fusion.4), channel_id=1, source_target_pairs={{0,1},{1,0},{2,3},{3,2},{4,5},{5,4},{6,7},{7,6},{8,9},{9,8},{10,11... | collective-permute-start | bytes 393224 | tf_op jit(solution)/shard_map/while/body/eval_jaxpr/ppermute | solution.py:10
  329.4 13.6 %collective-permute-start.1 = (bf16[128,512]{1,0:T(8,128)(2,1)S(1)}, bf16[128,512]{1,0:T(8,128)(2,1)S(1)}, u32[]{:S(2)}, u32[]{:S(2)}) collective-permute-start(bf16[128,512]{1,0:T(8,128)(2,1)S(1)} %broadcast_select_fusion.5), channel_id=1, source_target_pairs={{0,32},{1,33},{2,34},{3,35},{4,36},{5,37},{6,38},{7,39},{8,40},{9,... | collective-permute-start | bytes 393224 | tf_op jit(solution)/shard_map/while/body/eval_jaxpr/ppermute | solution.py:10
  343.3 18.4 %copy-start.10 = (f32[2,512]{1,0:T(2,128)S(1)}, f32[2,512]{1,0:T(2,128)}, u32[]{:S(2)}) copy-start(f32[2,512]{1,0:T(2,128)} %get-tuple-element.912) | copy-start | bytes 12292 | tf_op jit(solution)/shard_map/while
  343.3 18.4 %copy-start.12 = (f32[2,512]{1,0:T(2,128)S(1)}, f32[2,512]{1,0:T(2,128)}, u32[]{:S(2)}) copy-start(f32[2,512]{1,0:T(2,128)} %get-tuple-element.941) | copy-start | bytes 12292 | tf_op jit(solution)/shard_map/while
  343.4 18.4 %copy-start.18 = (s32[2,128]{1,0:T(2,128)S(1)}, s32[2,128]{1,0:T(2,128)}, u32[]{:S(2)}) copy-start(s32[2,128]{1,0:T(2,128)} %get-tuple-element.971) | copy-start | bytes 3076 | tf_op jit(solution)/shard_map/while
  345.9 15.8 %collective-permute-start.2 = (bf16[512,512]{1,0:T(8,128)(2,1)S(1)}, bf16[512,512]{1,0:T(8,128)(2,1)S(1)}, u32[]{:S(2)}, u32[]{:S(2)}) collective-permute-start(bf16[512,512]{1,0:T(8,128)(2,1)S(1)} %get-tuple-element.685), channel_id=1, source_target_pairs={{0,64},{64,128},{128,192},{1,65},{65,129},{129,193},{2,66},{66,130... | collective-permute-start | bytes 1572872 | tf_op jit(solution)/shard_map/while/body/eval_jaxpr/ppermute | solution.py:16
  366.0 12.7 %collective-permute-start = (bf16[128,512]{1,0:T(8,128)(2,1)}, bf16[128,512]{1,0:T(8,128)(2,1)S(1)}, u32[]{:S(2)}, u32[]{:S(2)}) collective-permute-start(bf16[128,512]{1,0:T(8,128)(2,1)} %broadcast_select_fusion.4), channel_id=1, source_target_pairs={{0,1},{1,0},{2,3},{3,2},{4,5},{5,4},{6,7},{7,6},{8,9},{9,8},{10,11... | collective-permute-start | bytes 393224 | tf_op jit(solution)/shard_map/while/body/eval_jaxpr/ppermute | solution.py:10
  388.5 13.6 %collective-permute-start.1 = (bf16[128,512]{1,0:T(8,128)(2,1)S(1)}, bf16[128,512]{1,0:T(8,128)(2,1)S(1)}, u32[]{:S(2)}, u32[]{:S(2)}) collective-permute-start(bf16[128,512]{1,0:T(8,128)(2,1)S(1)} %broadcast_select_fusion.5), channel_id=1, source_target_pairs={{0,32},{1,33},{2,34},{3,35},{4,36},{5,37},{6,38},{7,39},{8,40},{9,... | collective-permute-start | bytes 393224 | tf_op jit(solution)/shard_map/while/body/eval_jaxpr/ppermute | solution.py:10
  402.4 18.4 %copy-start.10 = (f32[2,512]{1,0:T(2,128)S(1)}, f32[2,512]{1,0:T(2,128)}, u32[]{:S(2)}) copy-start(f32[2,512]{1,0:T(2,128)} %get-tuple-element.912) | copy-start | bytes 12292 | tf_op jit(solution)/shard_map/while
  402.4 18.4 %copy-start.12 = (f32[2,512]{1,0:T(2,128)S(1)}, f32[2,512]{1,0:T(2,128)}, u32[]{:S(2)}) copy-start(f32[2,512]{1,0:T(2,128)} %get-tuple-element.941) | copy-start | bytes 12292 | tf_op jit(solution)/shard_map/while
  402.5 18.4 %copy-start.18 = (s32[2,128]{1,0:T(2,128)S(1)}, s32[2,128]{1,0:T(2,128)}, u32[]{:S(2)}) copy-start(s32[2,128]{1,0:T(2,128)} %get-tuple-element.971) | copy-start | bytes 3076 | tf_op jit(solution)/shard_map/while
  405.0 15.8 %collective-permute-start.2 = (bf16[512,512]{1,0:T(8,128)(2,1)S(1)}, bf16[512,512]{1,0:T(8,128)(2,1)S(1)}, u32[]{:S(2)}, u32[]{:S(2)}) collective-permute-start(bf16[512,512]{1,0:T(8,128)(2,1)S(1)} %get-tuple-element.685), channel_id=1, source_target_pairs={{0,64},{64,128},{128,192},{1,65},{65,129},{129,193},{2,66},{66,130... | collective-permute-start | bytes 1572872 | tf_op jit(solution)/shard_map/while/body/eval_jaxpr/ppermute | solution.py:16
  (104 other events, 392.0 us)
where the time goes:
time: 424 us; the launch traced here: 421 us
  waiting for transfers between devices  122 us (29%)
  local copies, waits for them, and re-layouts  80.1 us (19%)
  matrix products  79.6 us (19%)
  starting transfers between devices  75.6 us (18%)
  loops' own time  39.4 us (9%)
  other arithmetic  23.7 us (6%)
    ppermute x7, waiting for transfers between devices, shifted(): lax.ppermute(value, axis, [(source, source + steps) for source in range(l...  88.3 us
    ppermute x14, starting transfers between devices, from_partner(): lax.ppermute(x, axis, [(i, i ^ 1 << apart) for i in range(lax.axis_size(a...  53.4 us
    another operation x14, loops' own time, layer_step(): lax.fori_loop(0, most, slot_step, jnp.zeros(blocks.shape, jnp.float32))  37.4 us
    ppermute x14, waiting for transfers between devices, from_partner(): lax.ppermute(x, axis, [(i, i ^ 1 << apart) for i in range(lax.axis_size(a...  34 us
    dot_general x14, matrix products, layer_step(): z = z + jnp.dot(agg, weights[width:], preferred_element_type=jnp.float32)  30.8 us
    dot_general x14, matrix products, layer_step(): z = jnp.dot(x, weights[:width], preferred_element_type=jnp.float32)  27.6 us
    gather x42, local copies, waits for them, and re-layouts, slot_step(): source = jnp.take(blocks, cols, axis=0)  24.3 us
    ppermute x7, starting transfers between devices, shifted(): lax.ppermute(value, axis, [(source, source + steps) for source in range(l...  22.3 us
  transfers between devices with their start and end apart: 21, of which 14 were waited for; matrix products, arithmetic and copies ran while one was open for 15% of the time, Pallas kernels for 0%

commit v1 on v0

v1 whole, which is shorter than its diff:
```python
import functools

import jax
import jax.numpy as jnp
from jax import lax
from jax.experimental import pallas as pl
from jax.experimental.pallas import tpu as pltpu
from jax.sharding import PartitionSpec as P

LS = 2
X_CHIPS = 4
MESH = pl.DeviceIdType.MESH
F32 = jnp.float32
BF16 = jnp.bfloat16


def dot(a, b):
    return jnp.dot(a, b, preferred_element_type=F32)


def body(
    nseg,
    ndom,
    xc,
    feat,
    wts,
    bias,
    gain,
    tiles_hbm,
    cols,
    counts,
    cross_hbm,
    rows,
    out,
    wbuf,
    cbuf,
    small,
    hsec,
    hmid,
    xb,
    adj,
    tiles,
    snd,
    rcv,
    zp,
    loc_sem,
    ex_send,
    ex_recv,
    y_send,
    y_recv,
    c_send,
    c_recv,
    s_send,
    s_recv,
    x_send,
    x_recv,
    sib_send,
    sib_recv,
    o_send,
    o_recv,
    o_loc,
):
    s = lax.axis_index("segment")
    d = lax.axis_index("dom")
    core = d % 2
    xi = (d // 2) % xc
    base = d - (d % (2 * xc))
    sib = base + xi * 2 + (1 - core)
    anti = (d + ndom // 2) % ndom
    depth, width = wbuf.shape[1], wbuf.shape[2]
    nblk, nslot, tile = tiles_hbm.shape[0], tiles_hbm.shape[1], tiles_hbm.shape[2]
    nodes = nblk * tile
    bound = rows.shape[1]
    shard = depth // (2 * xc)
    mine = (xi * 2 + core) * shard

    def yid(dy):
        return ((s + dy) % nseg, d)

    def xid(dx):
        return (s, base + ((xi + dx) % xc) * 2 + core)

    load_h = pltpu.make_async_copy(feat.at[s], hsec.at[0], loc_sem.at[0])
    load_w = pltpu.make_async_copy(wts, wbuf.at[pl.ds(s * LS, LS)], loc_sem.at[1])
    load_c = pltpu.make_async_copy(cross_hbm, cbuf.at[pl.ds(s * LS, LS)], loc_sem.at[2])
    load_t = pltpu.make_async_copy(tiles_hbm, tiles, loc_sem.at[3])
    load_t.start()
    load_h.start()
    load_w.start()
    load_c.start()

    for i in range(LS):
        small[s * LS + i] = jnp.zeros((8, width), F32)
        small[s * LS + i, 0:1, :] = bias[i : i + 1, :]
        small[s * LS + i, 1:2, :] = gain[i : i + 1, :]
        small[s * LS + i, 2:3, 0:bound] = rows[i : i + 1, :].astype(F32)

    barrier = pltpu.get_barrier_semaphore()
    peers = [yid(dy) for dy in range(1, nseg)]
    peers += [xid(dx) for dx in range(1, xc)]
    peers += [(s, sib), (s, anti)]
    for peer in peers:
        pl.semaphore_signal(barrier, inc=1, device_id=peer, device_id_type=MESH)
    pl.semaphore_wait(barrier, len(peers))

    def remote(src, dst, send, recv, peer):
        return pltpu.make_async_remote_copy(
            src_ref=src,
            dst_ref=dst,
            send_sem=send,
            recv_sem=recv,
            device_id=peer,
            device_id_type=MESH,
        )

    def w_copy(i, l, dy):
        return remote(
            wts.at[i, pl.ds(mine, shard)],
            wbuf.at[l, pl.ds(mine, shard)],
            y_send.at[i, dy],
            y_recv.at[l],
            yid(dy),
        )

    def c_copy(i, l, dy):
        return remote(cross_hbm.at[i], cbuf.at[l], c_send.at[i, dy], c_recv.at[l], yid(dy))

    def s_copy(k, dy):
        part = small.at[pl.ds(k * LS, LS)]
        return remote(part, part, s_send.at[dy], s_recv.at[k], yid(dy))

    def x_copy(l, dx):
        part = wbuf.at[l, pl.ds(mine, shard)]
        return remote(part, part, x_send.at[l, dx], x_recv.at[l, dx], xid(dx))

    def x_from(l, dx):
        start = (((xi + xc - dx) % xc) * 2 + core) * shard
        return wbuf.at[l, pl.ds(start, shard)]

    def sib_copy(l, q):
        part = x_from(l, q)
        return remote(part, part, sib_send.at[l, q], sib_recv.at[l, q], (s, sib))

    def owner_sends(k):
        @pl.when(s == k)
        def _():
            for i in range(LS):
                for dy in range(1, nseg):
                    w_copy(i, k * LS + i, dy).start()
                if i == 0:
                    for dy in range(1, nseg):
                        s_copy(k, dy).start()
                for dy in range(1, nseg):
                    c_copy(i, k * LS + i, dy).start()

    def relay(k):
        @pl.when(s != k)
        def _():
            for i in range(LS):
                l = k * LS + i
                w_copy(i, l, 1).wait_recv()
                for dx in range(1, xc):
                    x_copy(l, dx).start()
                sib_copy(l, 0).start()
            for i in range(LS):
                l = k * LS + i
                for dx in range(1, xc):
                    x_copy(l, dx).wait_recv()
                    sib_copy(l, dx).start()

    def wait_weights(k, i):
        @pl.when(s != k)
        def _():
            l = k * LS + i
            for q in range(xc):
                sib_copy(l, q).wait_recv()
            c_copy(i, l, 1).wait_recv()

    def ex_copy(l, pos):
        peer = (s, sib) if pos == 0 else (s, anti)
        return remote(snd.at[l], rcv.at[l], ex_send.at[l], ex_recv.at[l], peer)

    def out_copy(k):
        dy = (k + nseg - s) % nseg
        return remote(hsec.at[k + 1], out.at[0, s], o_send.at[k], o_recv.at[dy], (k, d))

    def out_local(k):
        return pltpu.make_async_copy(hsec.at[k + 1], out.at[0, s], o_loc)

    owner_sends(0)

    load_t.wait()
    for r in range(nblk):
        for c in range(nblk):
            acc = jnp.zeros((tile, tile), F32)
            for k in range(nslot):
                live = (cols[r, k] == c) & (counts[r] > k)
                acc = acc + jnp.where(live, tiles[r, k].astype(F32), F32(0.0))
            adj[r * tile : (r + 1) * tile, c * tile : (c + 1) * tile] = acc.astype(BF16)
    load_h.wait()
    load_w.wait()
    load_c.wait()

    relay(0)

    def layer(k, pos, src, dst):
        l = k * LS + pos
        gain_row = small[l, 1:2, :]
        bias_row = small[l, 0:1, :]
        for r in range(0, nodes, 64):
            hf = src[r : r + 64, :].astype(F32)
            ms = jnp.mean(hf * hf, axis=-1, keepdims=True)
            xb[r : r + 64, :] = (hf * lax.rsqrt(ms + 1e-5) * gain_row).astype(BF16)
        listed = jnp.broadcast_to(small[l, 2:3, 0:bound], (bound, bound)).T
        lane = lax.broadcasted_iota(jnp.int32, (bound, bound), 1).astype(F32)
        sent = jnp.zeros((bound, width), F32)
        for c in range(0, nodes, bound):
            pick = jnp.where(listed == lane + F32(c), F32(1.0), F32(0.0)).astype(BF16)
            sent = sent + dot(pick, xb[c : c + bound, :])
        snd[l] = sent.astype(BF16)
        ex_copy(l, pos).start()
        wait_weights(k, pos)
        for r in range(0, nodes, tile):
            t = dot(adj[r : r + tile, :], xb[...]).astype(BF16)
            z = dot(xb[r : r + tile, :], wbuf[l, 0:width, :])
            zp[r : r + tile, :] = z + dot(t, wbuf[l, width:depth, :]) + bias_row
        if pos == LS - 1:

            @pl.when(k < nseg - 1)
            def _():
                relay(k + 1)

        ex_copy(l, pos).wait_recv()
        y = dot(rcv[l], wbuf[l, width:depth, :]).astype(BF16)
        for r in range(0, nodes, tile):
            z = zp[r : r + tile, :] + dot(cbuf[l, r : r + tile, :], y)
            half = z * F32(0.5)
            gate = half + half * jnp.tanh(half)
            dst[r : r + tile, :] = (src[r : r + tile, :].astype(F32) + gate).astype(BF16)

    def section(k, carry):
        owner_sends(k + 1)

        @pl.when(s != k)
        def _():
            s_copy(k, 1).wait_recv()

        layer(k, 0, hsec.at[k], hmid)
        layer(k, 1, hmid, hsec.at[k + 1])

        @pl.when(s == k)
        def _():
            out_local(k).start()

        @pl.when(s != k)
        def _():
            out_copy(k).start()

        return carry

    lax.fori_loop(0, nseg, section, 0)

    for i in range(LS):
        for dy in range(1, nseg):
            w_copy(i, s * LS + i, dy).wait_send()
            c_copy(i, s * LS + i, dy).wait_send()
    for dy in range(1, nseg):
        s_copy(s, dy).wait_send()

    def drain(k, carry):
        for i in range(LS):
            l = k * LS + i
            ex_copy(l, i).wait_send()

            @pl.when(s != k)
            def _():
                for q in range(xc):
                    sib_copy(l, q).wait_send()
                for dx in range(1, xc):
                    x_copy(l, dx).wait_send()

        @pl.when(s != k)
        def _():
            out_copy(k).wait_send()

        return carry

    lax.fori_loop(0, nseg, drain, 0)
    out_local(s).wait()
    for dy in range(1, nseg):
        from_seg = (s + nseg - dy) % nseg
        remote(
            hsec.at[0], out.at[0, from_seg], o_send.at[0], o_recv.at[dy], yid(dy)
        ).wait_recv()


def shards(nseg, ndom, xc, feat, wts, bias, gain, tiles, cols, counts, cross, rows):
    micro, nodes, width = feat.shape
    depth = wts.shape[1]
    nblk, nslot, tile = tiles.shape[0], tiles.shape[1], tiles.shape[2]
    bound = rows.shape[1]
    layers = LS * nseg
    cross = cross.reshape(LS, nodes, bound)
    dma = pltpu.SemaphoreType.DMA
    anyspec = pl.BlockSpec(memory_space=pl.ANY)
    vspec = pl.BlockSpec(memory_space=pltpu.VMEM)
    sspec = pl.BlockSpec(memory_space=pltpu.SMEM)
    return pl.pallas_call(
        functools.partial(body, nseg, ndom, xc),
        out_shape=jax.ShapeDtypeStruct((1, micro, nodes, width), BF16),
        in_specs=[anyspec, anyspec, vspec, vspec, anyspec, sspec, sspec, anyspec, vspec],
        out_specs=anyspec,
        scratch_shapes=[
            pltpu.VMEM((layers, depth, width), BF16),
            pltpu.VMEM((layers, nodes, bound), BF16),
            pltpu.VMEM((layers, 8, width), F32),
            pltpu.VMEM((nseg + 1, nodes, width), BF16),
            pltpu.VMEM((nodes, width), BF16),
            pltpu.VMEM((nodes, width), BF16),
            pltpu.VMEM((nodes, nodes), BF16),
            pltpu.VMEM((nblk, nslot, tile, tile), BF16),
            pltpu.VMEM((layers, bound, width), BF16),
            pltpu.VMEM((layers, bound, width), BF16),
            pltpu.VMEM((nodes, width), F32),
            dma((4,)),
            dma((layers,)),
            dma((layers,)),
            dma((LS, nseg)),
            dma((layers,)),
            dma((LS, nseg)),
            dma((layers,)),
            dma((nseg,)),
            dma((nseg,)),
            dma((layers, xc)),
            dma((layers, xc)),
            dma((layers, xc)),
            dma((layers, xc)),
            dma((nseg,)),
            dma((nseg,)),
            dma,
        ],
        compiler_params=pltpu.CompilerParams(
            collective_id=0, has_side_effects=True, vmem_limit_bytes=48 << 20
        ),
        name="relay",
    )(feat, wts, bias, gain, tiles, cols, counts, cross, rows)


def solution(mesh):
    in_specs = (
        P(None, "dom", None),
        P("segment", None, None),
        P("segment", None),
        P("segment", None),
        P("dom", None, None, None),
        P("dom", None),
        P("dom"),
        P("segment", "dom", None, None),
        P("segment", "dom"),
    )
    out_specs = P("segment", None, "dom", None)
    nseg, ndom = mesh.shape["segment"], mesh.shape["dom"]
    xc = X_CHIPS if ndom >= 4 * X_CHIPS else 2
    return jax.shard_map(
        functools.partial(shards, nseg, ndom, xc),
        mesh=mesh,
        in_specs=in_specs,
        out_specs=out_specs,
        check_vma=False,
    )
```

time: 424 us -> 164 us (0.39)
  the two profiles are of different devices: /device:TPU:86 before, /device:TPU:56 now
where the time goes in v1:
time: 164 us
  Pallas kernels  155 us (95%)
  local copies, waits for them, and re-layouts  8.29 us (5%)
    pallas_call x1, Pallas kernels, shards(): pl.pallas_call(functools.partial(body, nseg, ndom, xc), out_shape=jax.Sha...  155 us
    unnamed x17, local copies, waits for them, and re-layouts  8.29 us

profile of v1, /device:TPU:56, one launch (start us, length us, event | category | flops | bytes accessed | tf_op | source)
XLA Modules:
  0.0 163.8 jit_solution(16553982159881173735)
XLA Ops:
  0.0 0.0 copy-start
  0.0 1.6 copy-done
  1.6 0.0 copy-start.1
  1.6 1.0 copy-done.1
  2.6 0.0 copy-start.2
  2.6 0.9 copy-done.2
  3.6 0.0 copy-start.3
  3.6 0.7 copy-done.3
  4.3 0.0 copy-start.4
  4.3 0.7 copy-done.4
  5.0 0.0 copy-start.5
  5.0 0.7 copy-done.5
  5.6 0.0 copy-start.6
  5.6 0.7 copy-done.6
  6.3 0.0 copy-start.7
  6.3 0.7 copy-done.7
  7.0 155.5 %relay.1 = bf16[1,4,512,512]{3,2,1,0:T(8,128)(2,1)S(1)} custom-call(bf16[4,512,512]{2,1,0:T(8,128)(2,1)S(1)} %copy-done, bf16[2,1024,512]{2,1,0:T(8,128)(2,1)} %wts.1, f32[2,512]{1,0:T(2,128)S(1)} %copy-done.3, f32[2,512]{1,0:T(2,128)S(1)} %copy-done.4, bf16[4,4,128,128]{3,2,1,0:T(8,128)(2,1)S(1)} %copy-done.1, s32[4,4]{1,0:T(4,128)S(1)} %copy-done.5, ...), custom_call_target="tpu_custom_call" | custom-call | tf_op jit(solution)/shard_map/relay/pallas_call | solution.py:308
  162.4 1.3 copy.11
Async XLA Ops:
  0.0 1.6 copy-start
  1.6 1.0 copy-start.1
  2.6 0.9 copy-start.2
  3.6 0.7 copy-start.3
  4.3 0.7 copy-start.4
  5.0 0.7 copy-start.5
  5.6 0.7 copy-start.6
  6.3 0.7 copy-start.7

commit v2 on v1

--- a/solution.py
+++ b/solution.py
@@ -24,14 +24,17 @@
     xc,
     feat,
     wts,
-    bias,
-    gain,
+    bias_hbm,
+    gain_hbm,
     tiles_hbm,
     cols,
     counts,
     cross_hbm,
+    rows_hbm,
+    out,
+    bias,
+    gain,
     rows,
-    out,
     wbuf,
     cbuf,
     small,
@@ -84,11 +87,19 @@
     load_w = pltpu.make_async_copy(wts, wbuf.at[pl.ds(s * LS, LS)], loc_sem.at[1])
     load_c = pltpu.make_async_copy(cross_hbm, cbuf.at[pl.ds(s * LS, LS)], loc_sem.at[2])
     load_t = pltpu.make_async_copy(tiles_hbm, tiles, loc_sem.at[3])
+    loads = [
+        pltpu.make_async_copy(a, b, loc_sem.at[4 + i])
+        for i, (a, b) in enumerate(((bias_hbm, bias), (gain_hbm, gain), (rows_hbm, rows)))
+    ]
+    for load in loads:
+        load.start()
     load_t.start()
     load_h.start()
     load_w.start()
     load_c.start()
 
+    for load in loads:
+        load.wait()
     for i in range(LS):
         small[s * LS + i] = jnp.zeros((8, width), F32)
         small[s * LS + i, 0:1, :] = bias[i : i + 1, :]
@@ -153,20 +164,22 @@
                 for dy in range(1, nseg):
                     c_copy(i, k * LS + i, dy).start()
 
-    def relay(k):
-        @pl.when(s != k)
-        def _():
-            for i in range(LS):
-                l = k * LS + i
-                w_copy(i, l, 1).wait_recv()
-                for dx in range(1, xc):
-                    x_copy(l, dx).start()
-                sib_copy(l, 0).start()
-            for i in range(LS):
-                l = k * LS + i
-                for dx in range(1, xc):
-                    x_copy(l, dx).wait_recv()
-                    sib_copy(l, dx).start()
+    def spread(k, i):
+        @pl.when((s != k) & (k < nseg))
+        def _():
+            l = k * LS + i
+            w_copy(i, l, 1).wait_recv()
+            for dx in range(1, xc):
+                x_copy(l, dx).start()
+            sib_copy(l, 0).start()
+
+    def share(k, i):
+        @pl.when((s != k) & (k < nseg))
+        def _():
+            l = k * LS + i
+            for dx in range(1, xc):
+                x_copy(l, dx).wait_recv()
+                sib_copy(l, dx).start()
 
     def wait_weights(k, i):
         @pl.when(s != k)
@@ -180,12 +193,20 @@
         peer = (s, sib) if pos == 0 else (s, anti)
         return remote(snd.at[l], rcv.at[l], ex_send.at[l], ex_recv.at[l], peer)
 
-    def out_copy(k):
+    def out_copy(k, b):
         dy = (k + nseg - s) % nseg
-        return remote(hsec.at[k + 1], out.at[0, s], o_send.at[k], o_recv.at[dy], (k, d))
-
-    def out_local(k):
-        return pltpu.make_async_copy(hsec.at[k + 1], out.at[0, s], o_loc)
+        part = pl.ds(b * tile, tile)
+        return remote(
+            hsec.at[k + 1, part],
+            out.at[0, s, part],
+            o_send.at[k, b],
+            o_recv.at[dy, b],
+            (k, d),
+        )
+
+    def out_local(k, b):
+        part = pl.ds(b * tile, tile)
+        return pltpu.make_async_copy(hsec.at[k + 1, part], out.at[0, s, part], o_loc.at[b])
 
     owner_sends(0)
 
@@ -201,7 +222,19 @@
     load_w.wait()
     load_c.wait()
 
-    relay(0)
+    spread(0, 0)
+    owner_sends(1)
+    spread(0, 1)
+    share(0, 0)
+
+    def send_out(k, b):
+        @pl.when(s == k)
+        def _():
+            out_local(k, b).start()
+
+        @pl.when(s != k)
+        def _():
+            out_copy(k, b).start()
 
     def layer(k, pos, src, dst):
         l = k * LS + pos
@@ -224,12 +257,11 @@
             t = dot(adj[r : r + tile, :], xb[...]).astype(BF16)
             z = dot(xb[r : r + tile, :], wbuf[l, 0:width, :])
             zp[r : r + tile, :] = z + dot(t, wbuf[l, width:depth, :]) + bias_row
-        if pos == LS - 1:
-
-            @pl.when(k < nseg - 1)
-            def _():
-                relay(k + 1)
-
+        spread(k + 1, pos)
+        if pos < LS - 1:
+            share(k, pos + 1)
+        else:
+            share(k + 1, 0)
         ex_copy(l, pos).wait_recv()
         y = dot(rcv[l], wbuf[l, width:depth, :]).astype(BF16)
         for r in range(0, nodes, tile):
@@ -237,9 +269,11 @@
             half = z * F32(0.5)
             gate = half + half * jnp.tanh(half)
             dst[r : r + tile, :] = (src[r : r + tile, :].astype(F32) + gate).astype(BF16)
+            if pos == LS - 1:
+                send_out(k, r // tile)
 
     def section(k, carry):
-        owner_sends(k + 1)
+        owner_sends(k + 2)
 
         @pl.when(s != k)
         def _():
@@ -247,15 +281,6 @@
 
         layer(k, 0, hsec.at[k], hmid)
         layer(k, 1, hmid, hsec.at[k + 1])
-
-        @pl.when(s == k)
-        def _():
-            out_local(k).start()
-
-        @pl.when(s != k)
-        def _():
-            out_copy(k).start()
-
         return carry
 
     lax.fori_loop(0, nseg, section, 0)
@@ -281,17 +306,25 @@
 
         @pl.when(s != k)
         def _():
-            out_copy(k).wait_send()
+            for b in range(nblk):
+                out_copy(k, b).wait_send()
 
         return carry
 
     lax.fori_loop(0, nseg, drain, 0)
-    out_local(s).wait()
+    for b in range(nblk):
+        out_local(s, b).wait()
     for dy in range(1, nseg):
         from_seg = (s + nseg - dy) % nseg
-        remote(
-            hsec.at[0], out.at[0, from_seg], o_send.at[0], o_recv.at[dy], yid(dy)
-        ).wait_recv()
+        for b in range(nblk):
+            part = pl.ds(b * tile, tile)
+            remote(
+                hsec.at[0, part],
+                out.at[0, from_seg, part],
+                o_send.at[0, b],
+                o_recv.at[dy, b],
+                yid(dy),
+            ).wait_recv()
 
 
 def shards(nseg, ndom, xc, feat, wts, bias, gain, tiles, cols, counts, cross, rows):
@@ -302,15 +335,17 @@
     layers = LS * nseg
     cross = cross.reshape(LS, nodes, bound)
     dma = pltpu.SemaphoreType.DMA
-    anyspec = pl.BlockSpec(memory_space=pl.ANY)
-    vspec = pl.BlockSpec(memory_space=pltpu.VMEM)
+    anyspec = pl.BlockSpec(memory_space=pltpu.HBM)
     sspec = pl.BlockSpec(memory_space=pltpu.SMEM)
     return pl.pallas_call(
         functools.partial(body, nseg, ndom, xc),
         out_shape=jax.ShapeDtypeStruct((1, micro, nodes, width), BF16),
-        in_specs=[anyspec, anyspec, vspec, vspec, anyspec, sspec, sspec, anyspec, vspec],
-        out_specs=anyspec,
+        in_specs=[anyspec, anyspec, anyspec, anyspec, anyspec, sspec, sspec, anyspec, anyspec],
+        out_specs=pl.BlockSpec(memory_space=pl.ANY),
         scratch_shapes=[
+            pltpu.VMEM((LS, width), F32),
+            pltpu.VMEM((LS, width), F32),
+            pltpu.VMEM((LS, bound), jnp.int32),
             pltpu.VMEM((layers, depth, width), BF16),
             pltpu.VMEM((layers, nodes, bound), BF16),
             pltpu.VMEM((layers, 8, width), F32),
@@ -322,7 +357,7 @@
             pltpu.VMEM((layers, bound, width), BF16),
             pltpu.VMEM((layers, bound, width), BF16),
             pltpu.VMEM((nodes, width), F32),
-            dma((4,)),
+            dma((7,)),
             dma((layers,)),
             dma((layers,)),
             dma((LS, nseg)),
@@ -335,9 +370,9 @@
             dma((layers, xc)),
             dma((layers, xc)),
             dma((layers, xc)),
-            dma((nseg,)),
-            dma((nseg,)),
-            dma,
+            dma((nseg, nblk)),
+            dma((nseg, nblk)),
+            dma((nblk,)),
         ],
         compiler_params=pltpu.CompilerParams(
             collective_id=0, has_side_effects=True, vmem_limit_bytes=48 << 20

time: 164 us -> 121 us (0.74)
  the two profiles are of different devices: /device:TPU:56 before, /device:TPU:30 now
where the time goes in v2:
time: 121 us
  Pallas kernels  112 us (93%)
  local copies, waits for them, and re-layouts  8.29 us (7%)
    pallas_call x1, Pallas kernels, shards(): pl.pallas_call(functools.partial(body, nseg, ndom, xc), out_shape=jax.Sha...  112 us
    unnamed x17, local copies, waits for them, and re-layouts  8.29 us

profile of v2, /device:TPU:30, one launch (start us, length us, event | category | flops | bytes accessed | tf_op | source)
XLA Modules:
  0.0 120.8 jit_solution(12365853126393918297)
XLA Ops:
  0.0 0.0 copy-start
  0.0 1.6 %copy-done = bf16[4,512,512]{2,1,0:T(8,128)(2,1)S(1)} copy-done((bf16[4,512,512]{2,1,0:T(8,128)(2,1)S(1)}, bf16[4,512,512]{2,1,0:T(8,128)(2,1)}, u32[]{:S(2)}) %copy-start) | copy-done | bytes 2097176
  1.6 0.0 copy-start.1
  1.6 1.0 copy-done.1
  2.6 0.0 copy-start.2
  2.6 0.9 copy-done.2
  3.6 0.0 copy-start.3
  3.6 0.7 copy-done.3
  4.3 0.0 copy-start.4
  4.3 0.7 copy-done.4
  5.0 0.0 copy-start.5
  5.0 0.7 copy-done.5
  5.6 0.0 copy-start.6
  5.6 0.7 copy-done.6
  6.3 0.0 copy-start.7
  6.3 0.7 copy-done.7
  7.0 112.4 %relay.1 = bf16[1,4,512,512]{3,2,1,0:T(8,128)(2,1)S(1)} custom-call(bf16[4,512,512]{2,1,0:T(8,128)(2,1)S(1)} %copy-done, bf16[2,1024,512]{2,1,0:T(8,128)(2,1)} %wts.1, f32[2,512]{1,0:T(2,128)S(1)} %copy-done.3, f32[2,512]{1,0:T(2,128)S(1)} %copy-done.4, bf16[4,4,128,128]{3,2,1,0:T(8,128)(2,1)S(1)} %copy-done.1, s32[4,4]{1,0:T(4,128)S(1)} %copy-done.5, ...), custom_call_target="tpu_custom_call" | custom-call | tf_op jit(solution)/shard_map/relay/pallas_call | solution.py:340
  119.4 1.3 %copy.11 = bf16[1,4,512,512]{3,2,1,0:T(8,128)(2,1)} copy(bf16[1,4,512,512]{3,2,1,0:T(8,128)(2,1)S(1)} %relay.1) | data formatting | bytes 4194304
Async XLA Ops:
  0.0 1.6 %copy-start = (bf16[4,512,512]{2,1,0:T(8,128)(2,1)S(1)}, bf16[4,512,512]{2,1,0:T(8,128)(2,1)}, u32[]{:S(2)}) copy-start(bf16[4,512,512]{2,1,0:T(8,128)(2,1)} %feat.1) | copy-start | bytes 6291460
  1.6 1.0 copy-start.1
  2.6 0.9 copy-start.2
  3.6 0.7 copy-start.3
  4.3 0.7 copy-start.4
  5.0 0.7 copy-start.5
  5.6 0.7 copy-start.6
  6.3 0.7 copy-start.7

commit v3 on v2

--- a/solution.py
+++ b/solution.py
@@ -27,11 +27,13 @@
     bias_hbm,
     gain_hbm,
     tiles_hbm,
-    cols,
-    counts,
+    cols_hbm,
+    counts_hbm,
     cross_hbm,
     rows_hbm,
     out,
+    cols,
+    counts,
     bias,
     gain,
     rows,
@@ -89,7 +91,15 @@
     load_t = pltpu.make_async_copy(tiles_hbm, tiles, loc_sem.at[3])
     loads = [
         pltpu.make_async_copy(a, b, loc_sem.at[4 + i])
-        for i, (a, b) in enumerate(((bias_hbm, bias), (gain_hbm, gain), (rows_hbm, rows)))
+        for i, (a, b) in enumerate(
+            (
+                (bias_hbm, bias),
+                (gain_hbm, gain),
+                (rows_hbm, rows),
+                (cols_hbm, cols),
+                (counts_hbm, counts),
+            )
+        )
     ]
     for load in loads:
         load.start()
@@ -152,16 +162,19 @@
         part = x_from(l, q)
         return remote(part, part, sib_send.at[l, q], sib_recv.at[l, q], (s, sib))
 
+    order = sorted(range(1, nseg), key=lambda dy: min(dy, nseg - dy))
+
     def owner_sends(k):
         @pl.when(s == k)
         def _():
             for i in range(LS):
-                for dy in range(1, nseg):
+                for dy in order:
                     w_copy(i, k * LS + i, dy).start()
                 if i == 0:
-                    for dy in range(1, nseg):
+                    for dy in order:
                         s_copy(k, dy).start()
-                for dy in range(1, nseg):
+            for i in range(LS):
+                for dy in order:
                     c_copy(i, k * LS + i, dy).start()
 
     def spread(k, i):
@@ -327,6 +340,10 @@
             ).wait_recv()
 
 
+def hbm(a):
+    return pltpu.with_memory_space_constraint(a, pltpu.HBM)
+
+
 def shards(nseg, ndom, xc, feat, wts, bias, gain, tiles, cols, counts, cross, rows):
     micro, nodes, width = feat.shape
     depth = wts.shape[1]
@@ -336,13 +353,14 @@
     cross = cross.reshape(LS, nodes, bound)
     dma = pltpu.SemaphoreType.DMA
     anyspec = pl.BlockSpec(memory_space=pltpu.HBM)
-    sspec = pl.BlockSpec(memory_space=pltpu.SMEM)
     return pl.pallas_call(
         functools.partial(body, nseg, ndom, xc),
         out_shape=jax.ShapeDtypeStruct((1, micro, nodes, width), BF16),
-        in_specs=[anyspec, anyspec, anyspec, anyspec, anyspec, sspec, sspec, anyspec, anyspec],
+        in_specs=[anyspec] * 9,
         out_specs=pl.BlockSpec(memory_space=pl.ANY),
         scratch_shapes=[
+            pltpu.SMEM(cols.shape, jnp.int32),
+            pltpu.SMEM(counts.shape, jnp.int32),
             pltpu.VMEM((LS, width), F32),
             pltpu.VMEM((LS, width), F32),
             pltpu.VMEM((LS, bound), jnp.int32),
@@ -357,7 +375,7 @@
             pltpu.VMEM((layers, bound, width), BF16),
             pltpu.VMEM((layers, bound, width), BF16),
             pltpu.VMEM((nodes, width), F32),
-            dma((7,)),
+            dma((9,)),
             dma((layers,)),
             dma((layers,)),
             dma((LS, nseg)),
@@ -378,7 +396,7 @@
             collective_id=0, has_side_effects=True, vmem_limit_bytes=48 << 20
         ),
         name="relay",
-    )(feat, wts, bias, gain, tiles, cols, counts, cross, rows)
+    )(*(hbm(a) for a in (feat, wts, bias, gain, tiles, cols, counts, cross, rows)))
 
 
 def solution(mesh):

time: 121 us -> 107 us (0.88)
  the two profiles are of different devices: /device:TPU:30 before, /device:TPU:56 now
where the time goes in v3:
time: 107 us; the launch traced here: 105 us
  Pallas kernels  104 us (97%)
  local copies, waits for them, and re-layouts  1.32 us (1%)
    pallas_call x1, Pallas kernels, shards(): pl.pallas_call(functools.partial(body, nseg, ndom, xc), out_shape=jax.Sha...  104 us

profile of v3, /device:TPU:56, one launch (start us, length us, event | category | flops | bytes accessed | tf_op | source)
XLA Modules:
  0.0 105.4 jit_solution(723895730106077870)
XLA Ops:
  0.0 104.1 %relay.1 = bf16[1,4,512,512]{3,2,1,0:T(8,128)(2,1)S(1)} custom-call(bf16[4,512,512]{2,1,0:T(8,128)(2,1)} %feat.1, bf16[2,1024,512]{2,1,0:T(8,128)(2,1)} %wts.1, f32[2,512]{1,0:T(2,128)} %bias_hbm.1, f32[2,512]{1,0:T(2,128)} %gain_hbm.1, bf16[4,4,128,128]{3,2,1,0:T(8,128)(2,1)} %tiles_hbm.1, s32[4,4]{1,0:T(4,128)} %cols_hbm.1, s32[4]{0:T(128)} %counts_hbm.1, ...), custom_call_target="tpu_custom_call" | custom-call | tf_op jit(solution)/shard_map/relay/pallas_call | solution.py:356
  104.1 1.3 %copy.11 = bf16[1,4,512,512]{3,2,1,0:T(8,128)(2,1)} copy(bf16[1,4,512,512]{3,2,1,0:T(8,128)(2,1)S(1)} %relay.1) | data formatting | bytes 4194304

commit v4 on v3

--- a/solution.py
+++ b/solution.py
@@ -64,6 +64,8 @@
     o_send,
     o_recv,
     o_loc,
+    f_send,
+    f_recv,
 ):
     s = lax.axis_index("segment")
     d = lax.axis_index("dom")
@@ -165,6 +167,9 @@
     order = sorted(range(1, nseg), key=lambda dy: min(dy, nseg - dy))
 
     def owner_sends(k):
+        if isinstance(k, int) and k >= nseg:
+            return
+
         @pl.when(s == k)
         def _():
             for i in range(LS):
@@ -178,6 +183,9 @@
                     c_copy(i, k * LS + i, dy).start()
 
     def spread(k, i):
+        if isinstance(k, int) and k >= nseg:
+            return
+
         @pl.when((s != k) & (k < nseg))
         def _():
             l = k * LS + i
@@ -187,6 +195,9 @@
             sib_copy(l, 0).start()
 
     def share(k, i):
+        if isinstance(k, int) and k >= nseg:
+            return
+
         @pl.when((s != k) & (k < nseg))
         def _():
             l = k * LS + i
@@ -205,6 +216,19 @@
     def ex_copy(l, pos):
         peer = (s, sib) if pos == 0 else (s, anti)
         return remote(snd.at[l], rcv.at[l], ex_send.at[l], ex_recv.at[l], peer)
+
+    last = nseg - 1
+    far = (last + nseg // 2) % nseg
+
+    def far_copy(b):
+        part = pl.ds(b * tile, tile)
+        return remote(
+            hsec.at[last, part],
+            hsec.at[nseg + 1, part],
+            f_send.at[b],
+            f_recv.at[b],
+            (last, d),
+        )
 
     def out_copy(k, b):
         dy = (k + nseg - s) % nseg
@@ -220,6 +244,12 @@
     def out_local(k, b):
         part = pl.ds(b * tile, tile)
         return pltpu.make_async_copy(hsec.at[k + 1, part], out.at[0, s, part], o_loc.at[b])
+
+    def out_extra(b):
+        part = pl.ds(b * tile, tile)
+        return pltpu.make_async_copy(
+            hsec.at[nseg + 2, part], out.at[0, far, part], o_loc.at[nblk + b]
+        )
 
     owner_sends(0)
 
@@ -249,8 +279,13 @@
         def _():
             out_copy(k, b).start()
 
-    def layer(k, pos, src, dst):
+        @pl.when((s == far) & (k == last - 1))
+        def _():
+            far_copy(b).start()
+
+    def layer(k, pos, src, dst, extra=False):
         l = k * LS + pos
+        slot = LS * nseg + pos if extra else l
         gain_row = small[l, 1:2, :]
         bias_row = small[l, 0:1, :]
         for r in range(0, nodes, 64):
@@ -263,26 +298,30 @@
         for c in range(0, nodes, bound):
             pick = jnp.where(listed == lane + F32(c), F32(1.0), F32(0.0)).astype(BF16)
             sent = sent + dot(pick, xb[c : c + bound, :])
-        snd[l] = sent.astype(BF16)
-        ex_copy(l, pos).start()
-        wait_weights(k, pos)
+        snd[slot] = sent.astype(BF16)
+        ex_copy(slot, pos).start()
+        if not extra:
+            wait_weights(k, pos)
         for r in range(0, nodes, tile):
             t = dot(adj[r : r + tile, :], xb[...]).astype(BF16)
             z = dot(xb[r : r + tile, :], wbuf[l, 0:width, :])
             zp[r : r + tile, :] = z + dot(t, wbuf[l, width:depth, :]) + bias_row
-        spread(k + 1, pos)
-        if pos < LS - 1:
-            share(k, pos + 1)
-        else:
-            share(k + 1, 0)
-        ex_copy(l, pos).wait_recv()
-        y = dot(rcv[l], wbuf[l, width:depth, :]).astype(BF16)
+        if not extra:
+            spread(k + 1, pos)
+            if pos < LS - 1:
+                share(k, pos + 1)
+            else:
+                share(k + 1, 0)
+        ex_copy(slot, pos).wait_recv()
+        y = dot(rcv[slot], wbuf[l, width:depth, :]).astype(BF16)
         for r in range(0, nodes, tile):
             z = zp[r : r + tile, :] + dot(cbuf[l, r : r + tile, :], y)
             half = z * F32(0.5)
             gate = half + half * jnp.tanh(half)
             dst[r : r + tile, :] = (src[r : r + tile, :].astype(F32) + gate).astype(BF16)
-            if pos == LS - 1:
+            if extra and pos == LS - 1:
+                out_extra(r // tile).start()
+            elif pos == LS - 1:
                 send_out(k, r // tile)
 
     def section(k, carry):
@@ -296,7 +335,25 @@
         layer(k, 1, hmid, hsec.at[k + 1])
         return carry
 
-    lax.fori_loop(0, nseg, section, 0)
+    lax.fori_loop(0, last, section, 0)
+
+    @pl.when(s == far)
+    def _():
+        s_copy(last, 1).wait_recv()
+        wait_weights(last, 0)
+        share(last, 1)
+        wait_weights(last, 1)
+
+    @pl.when(s != far)
+    def _():
+        section(last, 0)
+
+    @pl.when(s == last)
+    def _():
+        for b in range(nblk):
+            far_copy(b).wait_recv()
+        layer(last, 0, hsec.at[nseg + 1], hmid, extra=True)
+        layer(last, 1, hmid, hsec.at[nseg + 2], extra=True)
 
     for i in range(LS):
         for dy in range(1, nseg):
@@ -308,7 +365,10 @@
     def drain(k, carry):
         for i in range(LS):
             l = k * LS + i
-            ex_copy(l, i).wait_send()
+
+            @pl.when((s != far) | (k != last))
+            def _():
+                ex_copy(l, i).wait_send()
 
             @pl.when(s != k)
             def _():
@@ -317,7 +377,7 @@
                 for dx in range(1, xc):
                     x_copy(l, dx).wait_send()
 
-        @pl.when(s != k)
+        @pl.when((s != k) & ((s != far) | (k != last)))
         def _():
             for b in range(nblk):
                 out_copy(k, b).wait_send()
@@ -325,19 +385,35 @@
         return carry
 
     lax.fori_loop(0, nseg, drain, 0)
+
+    @pl.when(s == far)
+    def _():
+        for b in range(nblk):
+            far_copy(b).wait_send()
+
+    @pl.when(s == last)
+    def _():
+        for i in range(LS):
+            ex_copy(LS * nseg + i, i).wait_send()
+        for b in range(nblk):
+            out_extra(b).wait()
+
     for b in range(nblk):
         out_local(s, b).wait()
     for dy in range(1, nseg):
         from_seg = (s + nseg - dy) % nseg
-        for b in range(nblk):
-            part = pl.ds(b * tile, tile)
-            remote(
-                hsec.at[0, part],
-                out.at[0, from_seg, part],
-                o_send.at[0, b],
-                o_recv.at[dy, b],
-                yid(dy),
-            ).wait_recv()
+
+        @pl.when((s != last) | (from_seg != far))
+        def _():
+            for b in range(nblk):
+                part = pl.ds(b * tile, tile)
+                remote(
+                    hsec.at[0, part],
+                    out.at[0, from_seg, part],
+                    o_send.at[0, b],
+                    o_recv.at[dy, b],
+                    yid(dy),
+                ).wait_recv()
 
 
 def hbm(a):
@@ -367,17 +443,17 @@
             pltpu.VMEM((layers, depth, width), BF16),
             pltpu.VMEM((layers, nodes, bound), BF16),
             pltpu.VMEM((layers, 8, width), F32),
-            pltpu.VMEM((nseg + 1, nodes, width), BF16),
+            pltpu.VMEM((nseg + 3, nodes, width), BF16),
             pltpu.VMEM((nodes, width), BF16),
             pltpu.VMEM((nodes, width), BF16),
             pltpu.VMEM((nodes, nodes), BF16),
             pltpu.VMEM((nblk, nslot, tile, tile), BF16),
-            pltpu.VMEM((layers, bound, width), BF16),
-            pltpu.VMEM((layers, bound, width), BF16),
+            pltpu.VMEM((layers + LS, bound, width), BF16),
+            pltpu.VMEM((layers + LS, bound, width), BF16),
             pltpu.VMEM((nodes, width), F32),
             dma((9,)),
-            dma((layers,)),
-            dma((layers,)),
+            dma((layers + LS,)),
+            dma((layers + LS,)),
             dma((LS, nseg)),
             dma((layers,)),
             dma((LS, nseg)),
@@ -390,6 +466,8 @@
             dma((layers, xc)),
             dma((nseg, nblk)),
             dma((nseg, nblk)),
+            dma((2 * nblk,)),
+            dma((nblk,)),
             dma((nblk,)),
         ],
         compiler_params=pltpu.CompilerParams(

time: 107 us -> 107 us (level)
  no operation moved by 1% of the time
where the time goes in v4:
time: 107 us; the launch traced here: 106 us
  Pallas kernels  104 us (97%)
  local copies, waits for them, and re-layouts  1.32 us (1%)
    pallas_call x1, Pallas kernels, shards(): pl.pallas_call(functools.partial(body, nseg, ndom, xc), out_shape=jax.Sha...  104 us

profile of v4, /device:TPU:56, one launch (start us, length us, event | category | flops | bytes accessed | tf_op | source)
XLA Modules:
  0.0 105.5 jit_solution(1750498042841612697)
XLA Ops:
  0.0 104.2 %relay.1 = bf16[1,4,512,512]{3,2,1,0:T(8,128)(2,1)S(1)} custom-call(bf16[4,512,512]{2,1,0:T(8,128)(2,1)} %feat.1, bf16[2,1024,512]{2,1,0:T(8,128)(2,1)} %wts.1, f32[2,512]{1,0:T(2,128)} %bias_hbm.1, f32[2,512]{1,0:T(2,128)} %gain_hbm.1, bf16[4,4,128,128]{3,2,1,0:T(8,128)(2,1)} %tiles_hbm.1, s32[4,4]{1,0:T(4,128)} %cols_hbm.1, s32[4]{0:T(128)} %counts_hbm.1, ...), custom_call_target="tpu_custom_call" | custom-call | tf_op jit(solution)/shard_map/relay/pallas_call | solution.py:432
  104.2 1.3 %copy.11 = bf16[1,4,512,512]{3,2,1,0:T(8,128)(2,1)} copy(bf16[1,4,512,512]{3,2,1,0:T(8,128)(2,1)S(1)} %relay.1) | data formatting | bytes 4194304

commit v5 on v4

--- a/solution.py
+++ b/solution.py
@@ -269,6 +269,7 @@
     owner_sends(1)
     spread(0, 1)
     share(0, 0)
+    owner_sends(2)
 
     def send_out(k, b):
         @pl.when(s == k)
@@ -325,13 +326,12 @@
                 send_out(k, r // tile)
 
     def section(k, carry):
-        owner_sends(k + 2)
-
         @pl.when(s != k)
         def _():
             s_copy(k, 1).wait_recv()
 
         layer(k, 0, hsec.at[k], hmid)
+        owner_sends(k + 3)
         layer(k, 1, hmid, hsec.at[k + 1])
         return carry
 

time: 107 us -> 95.8 us (0.90)
  the two profiles are of different devices: /device:TPU:56 before, /device:TPU:24 now
where the time goes in v5:
time: 95.8 us; the launch traced here: 95.7 us
  Pallas kernels  94.4 us (99%)
  local copies, waits for them, and re-layouts  1.32 us (1%)
    pallas_call x1, Pallas kernels, shards(): pl.pallas_call(functools.partial(body, nseg, ndom, xc), out_shape=jax.Sha...  94.4 us

profile of v5, /device:TPU:24, one launch (start us, length us, event | category | flops | bytes accessed | tf_op | source)
XLA Modules:
  0.0 95.7 jit_solution(17787810459089456779)
XLA Ops:
  0.0 94.4 %relay.1 = bf16[1,4,512,512]{3,2,1,0:T(8,128)(2,1)S(1)} custom-call(bf16[4,512,512]{2,1,0:T(8,128)(2,1)} %feat.1, bf16[2,1024,512]{2,1,0:T(8,128)(2,1)} %wts.1, f32[2,512]{1,0:T(2,128)} %bias_hbm.1, f32[2,512]{1,0:T(2,128)} %gain_hbm.1, bf16[4,4,128,128]{3,2,1,0:T(8,128)(2,1)} %tiles_hbm.1, s32[4,4]{1,0:T(4,128)} %cols_hbm.1, s32[4]{0:T(128)} %counts_hbm.1, ...), custom_call_target="tpu_custom_call" | custom-call | tf_op jit(solution)/shard_map/relay/pallas_call | solution.py:432
  94.4 1.3 %copy.11 = bf16[1,4,512,512]{3,2,1,0:T(8,128)(2,1)} copy(bf16[1,4,512,512]{3,2,1,0:T(8,128)(2,1)S(1)} %relay.1) | data formatting | bytes 4194304

commit v6 on v5

--- a/solution.py
+++ b/solution.py
@@ -48,6 +48,8 @@
     snd,
     rcv,
     zp,
+    tb,
+    picks,
     loc_sem,
     ex_send,
     ex_recv,
@@ -80,12 +82,22 @@
     bound = rows.shape[1]
     shard = depth // (2 * xc)
     mine = (xi * 2 + core) * shard
+    halves = 2
+    half_shard = shard // halves
+    rstep, nstep = min(256, nodes), min(256, width)
 
     def yid(dy):
         return ((s + dy) % nseg, d)
 
     def xid(dx):
         return (s, base + ((xi + dx) % xc) * 2 + core)
+
+    barrier = pltpu.get_barrier_semaphore()
+    peers = [yid(dy) for dy in range(1, nseg)]
+    peers += [xid(dx) for dx in range(1, xc)]
+    peers += [(s, sib), (s, anti)]
+    for peer in peers:
+        pl.semaphore_signal(barrier, inc=1, device_id=peer, device_id_type=MESH)
 
     load_h = pltpu.make_async_copy(feat.at[s], hsec.at[0], loc_sem.at[0])
     load_w = pltpu.make_async_copy(wts, wbuf.at[pl.ds(s * LS, LS)], loc_sem.at[1])
@@ -118,12 +130,6 @@
         small[s * LS + i, 1:2, :] = gain[i : i + 1, :]
         small[s * LS + i, 2:3, 0:bound] = rows[i : i + 1, :].astype(F32)
 
-    barrier = pltpu.get_barrier_semaphore()
-    peers = [yid(dy) for dy in range(1, nseg)]
-    peers += [xid(dx) for dx in range(1, xc)]
-    peers += [(s, sib), (s, anti)]
-    for peer in peers:
-        pl.semaphore_signal(barrier, inc=1, device_id=peer, device_id_type=MESH)
     pl.semaphore_wait(barrier, len(peers))
 
     def remote(src, dst, send, recv, peer):
@@ -136,12 +142,13 @@
             device_id_type=MESH,
         )
 
-    def w_copy(i, l, dy):
+    def w_copy(i, l, dy, h):
+        part = pl.ds(mine + h * half_shard, half_shard)
         return remote(
-            wts.at[i, pl.ds(mine, shard)],
-            wbuf.at[l, pl.ds(mine, shard)],
-            y_send.at[i, dy],
-            y_recv.at[l],
+            wts.at[i, part],
+            wbuf.at[l, part],
+            y_send.at[i, dy, h],
+            y_recv.at[l, h],
             yid(dy),
         )
 
@@ -152,9 +159,9 @@
         part = small.at[pl.ds(k * LS, LS)]
         return remote(part, part, s_send.at[dy], s_recv.at[k], yid(dy))
 
-    def x_copy(l, dx):
-        part = wbuf.at[l, pl.ds(mine, shard)]
-        return remote(part, part, x_send.at[l, dx], x_recv.at[l, dx], xid(dx))
+    def x_copy(l, dx, h):
+        part = wbuf.at[l, pl.ds(mine + h * half_shard, half_shard)]
+        return remote(part, part, x_send.at[l, dx, h], x_recv.at[l, dx, h], xid(dx))
 
     def x_from(l, dx):
         start = (((xi + xc - dx) % xc) * 2 + core) * shard
@@ -173,8 +180,9 @@
         @pl.when(s == k)
         def _():
             for i in range(LS):
-                for dy in order:
-                    w_copy(i, k * LS + i, dy).start()
+                for h in range(halves):
+                    for dy in order:
+                        w_copy(i, k * LS + i, dy, h).start()
                 if i == 0:
                     for dy in order:
                         s_copy(k, dy).start()
@@ -189,9 +197,10 @@
         @pl.when((s != k) & (k < nseg))
         def _():
             l = k * LS + i
-            w_copy(i, l, 1).wait_recv()
-            for dx in range(1, xc):
-                x_copy(l, dx).start()
+            for h in range(halves):
+                w_copy(i, l, 1, h).wait_recv()
+                for dx in range(1, xc):
+                    x_copy(l, dx, h).start()
             sib_copy(l, 0).start()
 
     def share(k, i):
@@ -202,7 +211,8 @@
         def _():
             l = k * LS + i
             for dx in range(1, xc):
-                x_copy(l, dx).wait_recv()
+                for h in range(halves):
+                    x_copy(l, dx, h).wait_recv()
                 sib_copy(l, dx).start()
 
     def wait_weights(k, i):
@@ -265,11 +275,6 @@
     load_w.wait()
     load_c.wait()
 
-    spread(0, 0)
-    owner_sends(1)
-    spread(0, 1)
-    share(0, 0)
-    owner_sends(2)
 
     def send_out(k, b):
         @pl.when(s == k)
@@ -283,63 +288,92 @@
         @pl.when((s == far) & (k == last - 1))
         def _():
             far_copy(b).start()
+
+    def norm(hf, gain_row):
+        ms = jnp.mean(hf * hf, axis=-1, keepdims=True)
+        return (hf * lax.rsqrt(ms + 1e-5) * gain_row).astype(BF16)
+
+    def make_x(src, l):
+        gain_row = small[l, 1:2, :]
+        for r in range(0, nodes, 64):
+            xb[r : r + 64, :] = norm(src[r : r + 64, :].astype(F32), gain_row)
+
+    def make_pick(l, pos):
+        listed = jnp.broadcast_to(small[l, 2:3, 0:bound], (bound, bound)).T
+        lane = lax.broadcasted_iota(jnp.int32, (bound, bound), 1).astype(F32)
+        for c in range(0, nodes, bound):
+            hit = jnp.where(listed == lane + F32(c), F32(1.0), F32(0.0))
+            picks[pos, :, c : c + bound] = hit.astype(BF16)
 
     def layer(k, pos, src, dst, extra=False):
         l = k * LS + pos
         slot = LS * nseg + pos if extra else l
-        gain_row = small[l, 1:2, :]
-        bias_row = small[l, 0:1, :]
-        for r in range(0, nodes, 64):
-            hf = src[r : r + 64, :].astype(F32)
-            ms = jnp.mean(hf * hf, axis=-1, keepdims=True)
-            xb[r : r + 64, :] = (hf * lax.rsqrt(ms + 1e-5) * gain_row).astype(BF16)
-        listed = jnp.broadcast_to(small[l, 2:3, 0:bound], (bound, bound)).T
-        lane = lax.broadcasted_iota(jnp.int32, (bound, bound), 1).astype(F32)
-        sent = jnp.zeros((bound, width), F32)
-        for c in range(0, nodes, bound):
-            pick = jnp.where(listed == lane + F32(c), F32(1.0), F32(0.0)).astype(BF16)
-            sent = sent + dot(pick, xb[c : c + bound, :])
-        snd[slot] = sent.astype(BF16)
+        final = isinstance(k, int) and k == last
+        follow = pos < LS - 1 or not final
+        snd[slot] = dot(picks[pos], xb[...]).astype(BF16)
         ex_copy(slot, pos).start()
+        for r in range(0, nodes, rstep):
+            tb[r : r + rstep, :] = dot(adj[r : r + rstep, :], xb[...]).astype(BF16)
         if not extra:
             wait_weights(k, pos)
-        for r in range(0, nodes, tile):
-            t = dot(adj[r : r + tile, :], xb[...]).astype(BF16)
-            z = dot(xb[r : r + tile, :], wbuf[l, 0:width, :])
-            zp[r : r + tile, :] = z + dot(t, wbuf[l, width:depth, :]) + bias_row
+        bias_row = small[l, 0:1, :]
+        for n in range(0, width, nstep):
+            for r in range(0, nodes, rstep):
+                z = dot(xb[r : r + rstep, :], wbuf[l, 0:width, n : n + nstep])
+                z = z + dot(tb[r : r + rstep, :], wbuf[l, width:depth, n : n + nstep])
+                zp[r : r + rstep, n : n + nstep] = z + bias_row[:, n : n + nstep]
         if not extra:
             spread(k + 1, pos)
             if pos < LS - 1:
                 share(k, pos + 1)
+                make_pick(l + 1, pos + 1)
             else:
                 share(k + 1, 0)
+                if follow:
+
+                    @pl.when(s != k + 1)
+                    def _():
+                        s_copy(k + 1, 1).wait_recv()
+
+                    make_pick(l + 1, 0)
         ex_copy(slot, pos).wait_recv()
         y = dot(rcv[slot], wbuf[l, width:depth, :]).astype(BF16)
         for r in range(0, nodes, tile):
             z = zp[r : r + tile, :] + dot(cbuf[l, r : r + tile, :], y)
             half = z * F32(0.5)
             gate = half + half * jnp.tanh(half)
-            dst[r : r + tile, :] = (src[r : r + tile, :].astype(F32) + gate).astype(BF16)
+            hb = (src[r : r + tile, :].astype(F32) + gate).astype(BF16)
+            dst[r : r + tile, :] = hb
+            if follow:
+                xb[r : r + tile, :] = norm(hb.astype(F32), small[l + 1, 1:2, :])
             if extra and pos == LS - 1:
                 out_extra(r // tile).start()
             elif pos == LS - 1:
                 send_out(k, r // tile)
 
     def section(k, carry):
-        @pl.when(s != k)
-        def _():
-            s_copy(k, 1).wait_recv()
-
         layer(k, 0, hsec.at[k], hmid)
         owner_sends(k + 3)
         layer(k, 1, hmid, hsec.at[k + 1])
         return carry
 
+    spread(0, 0)
+    owner_sends(1)
+
+    @pl.when(s != 0)
+    def _():
+        s_copy(0, 1).wait_recv()
+
+    make_x(hsec.at[0], 0)
+    make_pick(0, 0)
+    spread(0, 1)
+    share(0, 0)
+    owner_sends(2)
+
     lax.fori_loop(0, last, section, 0)
 
     @pl.when(s == far)
     def _():
-        s_copy(last, 1).wait_recv()
         wait_weights(last, 0)
         share(last, 1)
         wait_weights(last, 1)
@@ -352,12 +386,14 @@
     def _():
         for b in range(nblk):
             far_copy(b).wait_recv()
+        make_x(hsec.at[nseg + 1], last * LS)
         layer(last, 0, hsec.at[nseg + 1], hmid, extra=True)
         layer(last, 1, hmid, hsec.at[nseg + 2], extra=True)
 
     for i in range(LS):
         for dy in range(1, nseg):
-            w_copy(i, s * LS + i, dy).wait_send()
+            for h in range(halves):
+                w_copy(i, s * LS + i, dy, h).wait_send()
             c_copy(i, s * LS + i, dy).wait_send()
     for dy in range(1, nseg):
         s_copy(s, dy).wait_send()
@@ -375,7 +411,8 @@
                 for q in range(xc):
                     sib_copy(l, q).wait_send()
                 for dx in range(1, xc):
-                    x_copy(l, dx).wait_send()
+                    for h in range(halves):
+                        x_copy(l, dx, h).wait_send()
 
         @pl.when((s != k) & ((s != far) | (k != last)))
         def _():
@@ -451,17 +488,19 @@
             pltpu.VMEM((layers + LS, bound, width), BF16),
             pltpu.VMEM((layers + LS, bound, width), BF16),
             pltpu.VMEM((nodes, width), F32),
+            pltpu.VMEM((nodes, width), BF16),
+            pltpu.VMEM((LS, bound, nodes), BF16),
             dma((9,)),
             dma((layers + LS,)),
             dma((layers + LS,)),
-            dma((LS, nseg)),
-            dma((layers,)),
+            dma((LS, nseg, 2)),
+            dma((layers, 2)),
             dma((LS, nseg)),
             dma((layers,)),
             dma((nseg,)),
             dma((nseg,)),
-            dma((layers, xc)),
-            dma((layers, xc)),
+            dma((layers, xc, 2)),
+            dma((layers, xc, 2)),
             dma((layers, xc)),
             dma((layers, xc)),
             dma((nseg, nblk)),

time: 95.8 us -> 94.8 us (0.990)
  the two profiles are of different devices: /device:TPU:24 before, /device:TPU:56 now
where the time goes in v6:
time: 94.8 us; the launch traced here: 94.7 us
  Pallas kernels  93.4 us (99%)
  local copies, waits for them, and re-layouts  1.32 us (1%)
    pallas_call x1, Pallas kernels, shards(): pl.pallas_call(functools.partial(body, nseg, ndom, xc), out_shape=jax.Sha...  93.4 us

profile of v6, /device:TPU:56, one launch (start us, length us, event | category | flops | bytes accessed | tf_op | source)
XLA Modules:
  0.0 94.7 jit_solution(8688585192110636018)
XLA Ops:
  0.0 93.4 %relay.1 = bf16[1,4,512,512]{3,2,1,0:T(8,128)(2,1)S(1)} custom-call(bf16[4,512,512]{2,1,0:T(8,128)(2,1)} %feat.1, bf16[2,1024,512]{2,1,0:T(8,128)(2,1)} %wts.1, f32[2,512]{1,0:T(2,128)} %bias_hbm.1, f32[2,512]{1,0:T(2,128)} %gain_hbm.1, bf16[4,4,128,128]{3,2,1,0:T(8,128)(2,1)} %tiles_hbm.1, s32[4,4]{1,0:T(4,128)} %cols_hbm.1, s32[4]{0:T(128)} %counts_hbm.1, ...), custom_call_target="tpu_custom_call" | custom-call | tf_op jit(solution)/shard_map/relay/pallas_call | solution.py:469
  93.4 1.3 %copy.11 = bf16[1,4,512,512]{3,2,1,0:T(8,128)(2,1)} copy(bf16[1,4,512,512]{3,2,1,0:T(8,128)(2,1)S(1)} %relay.1) | data formatting | bytes 4194304

commit v7 on v6

--- a/solution.py
+++ b/solution.py
@@ -180,8 +180,9 @@
         @pl.when(s == k)
         def _():
             for i in range(LS):
+                first = order[::-1] if isinstance(k, int) and k == 0 else order
                 for h in range(halves):
-                    for dy in order:
+                    for dy in first:
                         w_copy(i, k * LS + i, dy, h).start()
                 if i == 0:
                     for dy in order:

time: 94.8 us -> 94.8 us (level)
  no operation moved by 1% of the time
where the time goes in v7:
time: 94.8 us; the launch traced here: 94.7 us
  Pallas kernels  93.4 us (99%)
  local copies, waits for them, and re-layouts  1.32 us (1%)
    pallas_call x1, Pallas kernels, shards(): pl.pallas_call(functools.partial(body, nseg, ndom, xc), out_shape=jax.Sha...  93.4 us

profile of v7, /device:TPU:56, one launch (start us, length us, event | category | flops | bytes accessed | tf_op | source)
XLA Modules:
  0.0 94.7 jit_solution(5772393044622630623)
XLA Ops:
  0.0 93.4 %relay.1 = bf16[1,4,512,512]{3,2,1,0:T(8,128)(2,1)S(1)} custom-call(bf16[4,512,512]{2,1,0:T(8,128)(2,1)} %feat.1, bf16[2,1024,512]{2,1,0:T(8,128)(2,1)} %wts.1, f32[2,512]{1,0:T(2,128)} %bias_hbm.1, f32[2,512]{1,0:T(2,128)} %gain_hbm.1, bf16[4,4,128,128]{3,2,1,0:T(8,128)(2,1)} %tiles_hbm.1, s32[4,4]{1,0:T(4,128)} %cols_hbm.1, s32[4]{0:T(128)} %counts_hbm.1, ...), custom_call_target="tpu_custom_call" | custom-call | tf_op jit(solution)/shard_map/relay/pallas_call | solution.py:470
  93.4 1.3 %copy.11 = bf16[1,4,512,512]{3,2,1,0:T(8,128)(2,1)} copy(bf16[1,4,512,512]{3,2,1,0:T(8,128)(2,1)S(1)} %relay.1) | data formatting | bytes 4194304
